TPU v7x, 128 devices: a whole 4x4x4 slice. The times are simulated.
128 devices in a mesh: clip: 8 (over x, core), tok: 16 (over y, z).
Axes of the slice: x: 4, y: 4, z: 4, core: 2. Of those that a mesh axis runs over, the one named last changes fastest.
Arguments:
- tokens: bfloat16 [65536, 1024], P(('clip', 'tok')), may hold values from -80 to 80
- slot_keys: bfloat16 [1024, 1024], replicated, may hold values from -64 to 64
- w_in: bfloat16 [16, 1024, 4096], P('tok', None, 'clip'), may hold values from -0.1875 to 0.1875
- w_back: bfloat16 [16, 4096, 1024], P('tok', 'clip'), may hold values from -0.09375 to 0.09375
- w_proj: bfloat16 [1024, 512], replicated, may hold values from -0.1875 to 0.1875
- dec_source: int32 [8, 4096], P('clip'), may hold values from 0 to 8192, as said below
- mask_token: bfloat16 [512], replicated, may hold values from -80 to 80
- w_qkv: bfloat16 [512, 1536], replicated, may hold values from -8 to 8
- w_out: bfloat16 [512, 512], replicated, may hold values from -9 to 9
Outputs:
- decoded: bfloat16 [32768, 512], P(('clip', 'tok'))
Inputs may be any that keep to these rules, and one draw needn't show every extreme that they name: `dec_source`: within a clip no visible index appears twice. For each aligned block of 256 decoder positions and each aligned block of 512 visible tokens, at most 16 positions of the first show tokens of the second, and some pair of blocks reaches 16 in every clip.
All inputs are finite; a program needn't handle non-finite values.
Results may differ from a plain program's by a relative error of at most 0.025.
Values may be sent and summed in bfloat16 or wider, within the bound.
A program may use at most 64 MiB of HBM per device.

v0:
```python
import math

import jax
import jax.numpy as jnp
from jax import lax
from jax.sharding import PartitionSpec as P

HEADS = 16


def layer_norm(values):
    centre = values - jnp.mean(values, axis=-1, keepdims=True)
    spread = jnp.mean(centre * centre, axis=-1, keepdims=True)
    return centre * lax.rsqrt(spread + 1e-05)


def sinusoid(places, width):
    half = width // 2
    speeds = jnp.exp(-math.log(10000.0) * jnp.arange(half).astype(jnp.float32) / half)
    angles = places.astype(jnp.float32)[:, None] * speeds[None, :]
    return jnp.concatenate([jnp.sin(angles), jnp.cos(angles)], axis=1)


def attend(queries, key_rows, value_rows):
    heads_here, head_dim, count = queries.shape
    block = math.gcd(count, 512)
    scale = 1.0 / math.sqrt(head_dim)
    blocks = queries.reshape(heads_here, head_dim, count // block, block).transpose(2, 0, 1, 3)

    def one_block(query_block):
        scores = (
            jnp.einsum("hkq,hkn->hqn", query_block, key_rows, preferred_element_type=jnp.float32)
            * scale
        )
        highest = jnp.max(scores, axis=-1)
        raised = jnp.exp(scores - highest[..., None]).astype(jnp.bfloat16)
        totals = jnp.sum(raised.astype(jnp.float32), axis=-1)
        summed = jnp.einsum("hqn,hkn->hkq", raised, value_rows, preferred_element_type=jnp.float32)
        return (summed / totals[:, None, :]).astype(jnp.bfloat16)

    outcome = lax.map(one_block, blocks)
    return outcome.transpose(1, 2, 0, 3).reshape(heads_here, head_dim, count)


def per_device(tokens, slot_keys, w_in, w_back, w_proj, dec_source, mask_token, w_qkv, w_out):
    vis_dev, width = tokens.shape
    n_tok = lax.axis_size("tok")
    dec_width = w_proj.shape[1]
    normed = layer_norm(tokens.astype(jnp.float32)).astype(jnp.bfloat16)
    logits = jnp.dot(normed, slot_keys, preferred_element_type=jnp.float32)
    col_top = lax.pmax(jnp.max(logits, axis=0), "tok")
    dispatch = jnp.exp(logits - col_top[None, :]).astype(jnp.bfloat16)
    slot_sums = lax.dot_general(
        dispatch, normed, (((0,), (0,)), ((), ())), preferred_element_type=jnp.float32
    )
    slot_totals = jnp.sum(dispatch.astype(jnp.float32), axis=0)
    mine_sums, mine_totals = (
        lax.psum_scatter(slot_sums, "tok", scatter_dimension=0, tiled=True),
        lax.psum_scatter(slot_totals, "tok", scatter_dimension=0, tiled=True),
    )
    slot_in = (mine_sums / mine_totals[:, None]).astype(jnp.bfloat16)
    first_proj = w_in[0]
    second_proj = w_back[0]
    hidden = jax.nn.gelu(
        jnp.dot(
            lax.all_gather(slot_in, "clip", axis=0, tiled=True),
            first_proj,
            preferred_element_type=jnp.float32,
        )
    ).astype(jnp.bfloat16)
    partial_out = jnp.dot(hidden, second_proj, preferred_element_type=jnp.float32)
    slot_out = lax.psum_scatter(partial_out, "clip", scatter_dimension=0, tiled=True).astype(
        jnp.bfloat16
    )
    row_top = jnp.max(logits, axis=1, keepdims=True)
    raised = jnp.exp(logits - row_top)
    combine = (raised / jnp.sum(raised, axis=1, keepdims=True)).astype(jnp.bfloat16)
    moe = jnp.dot(
        combine,
        lax.all_gather(slot_out, "tok", axis=0, tiled=True),
        preferred_element_type=jnp.float32,
    ).astype(jnp.bfloat16)
    projected = jnp.dot(moe, w_proj, preferred_element_type=jnp.float32).astype(jnp.bfloat16)
    listing = dec_source[0]
    dec_total = listing.shape[0]
    dec_dev = dec_total // n_tok
    vis_all = vis_dev * n_tok
    myself = lax.axis_index("tok")
    own_list = lax.dynamic_slice_in_dim(listing, myself * dec_dev, dec_dev)
    visible = own_list < vis_all
    places = myself * dec_dev + jnp.arange(dec_dev)
    filler = (mask_token.astype(jnp.float32)[None, :] + sinusoid(places, dec_width)).astype(
        jnp.bfloat16
    )
    everyone = lax.all_gather(projected, "tok", axis=0, tiled=True)
    picked = jnp.take(everyone, jnp.minimum(own_list, vis_all - 1), axis=0)
    dec_in = jnp.where(visible[:, None], picked, filler)
    head_dim = dec_width // HEADS
    dec_normed = layer_norm(dec_in.astype(jnp.float32)).astype(jnp.bfloat16)
    qkv = jnp.einsum(
        "pd,dchk->chkp",
        dec_normed,
        w_qkv.reshape(dec_width, 3, HEADS, head_dim),
        preferred_element_type=jnp.float32,
    ).astype(jnp.bfloat16)
    spread = lax.all_to_all(qkv, "tok", split_axis=1, concat_axis=3, tiled=True)
    attended = attend(spread[0], spread[1], spread[2])
    attended = lax.all_to_all(attended, "tok", split_axis=2, concat_axis=0, tiled=True)
    mixed = jnp.einsum(
        "hkp,hke->pe",
        attended,
        w_out.reshape(HEADS, head_dim, dec_width),
        preferred_element_type=jnp.float32,
    )
    return (mixed + dec_in.astype(jnp.float32)).astype(jnp.bfloat16)


def solution(mesh):
    placed = (
        P(("clip", "tok"), None),
        P(),
        P("tok", None, "clip"),
        P("tok", "clip", None),
        P(),
        P("clip", None),
        P(),
        P(),
        P(),
    )
    return jax.shard_map(
        per_device, mesh=mesh, in_specs=placed, out_specs=P(("clip", "tok"), None), check_vma=False
    )
```

profile of v0, /device:TPU:0, one launch (start us, length us, event | category | flops | bytes accessed | tf_op | source)
XLA Modules:
  0.0 457.1 jit_solution(16553922433638070908)
XLA Ops:
  9.8 2.6 fusion.59
  12.4 42.0 %pmax.7 = f32[1024]{0:T(1024)S(1)} all-reduce(f32[1024]{0:T(1024)S(1)} %get-tuple-element.46), channel_id=1, replica_groups=mesh['clip'=8,'tok'=16] {'tok'}, use_global_device_ids=true, to_apply=%region_5.0 | all-reduce | flops 1024 | bytes 8192 | tf_op jit(solution)/shard_map/pmax | solution.py:51
  54.5 5.0 %fusion.46 = f32[1024,1024]{1,0:T(8,128)} fusion(f32[512,1024]{1,0:T(8,128)} %get-tuple-element.70, f32[1024]{0:T(1024)S(1)} %pmax.7, bf16[512,1024]{1,0:T(8,128)(2,1)S(1)} %copy-done.1, f32[512]{0:T(512)S(1)} %add_rsqrt_fusion, f32[512]{0:T(512)S(1)} %broadcast_multiply_fusion), kind=kOutput, calls=%fused_computation.61 | convolution fusion | flops 1076887552 | bytes 7348224 | tf_op jit(solution)/shard_map/dot_general | solution.py:53
  61.3 2.3 fusion.13
  63.7 35.8 %all-reduce = f32[1024]{0:T(1024)S(1)} all-reduce(f32[1024]{0:T(1024)S(1)} %get-tuple-element.44), channel_id=3, replica_groups=mesh['clip'=8,'tok'=16] {'tok'}, use_global_device_ids=true, to_apply=%region_8.0.clone | all-reduce | flops 1024 | bytes 8192
  99.5 35.1 %reduce-scatter.3.cloned.1.call-done = f32[64,1024]{1,0:T(8,128)} async-done(((f32[1024,1024]{1,0:T(8,128)}), f32[64,1024]{1,0:T(8,128)}) %reduce-scatter.3.cloned.1.call-update) | async-done | bytes 262160 | tf_op jit(solution)/shard_map/reduce_scatter | solution.py:58
  136.3 22.4 %all-gather.4.cloned.1.call-done = bf16[512,1024]{1,0:T(8,128)(2,1)} async-done(((bf16[64,1024]{1,0:T(8,128)(2,1)}), bf16[512,1024]{1,0:T(8,128)(2,1)}) %all-gather.4.cloned.1.call-update) | async-done | bytes 1048592 | tf_op jit(solution)/shard_map/all_gather | solution.py:66
  158.7 4.6 %fusion.24 = f32[512,1024]{1,0:T(8,128)} fusion(bf16[1,512,1024]{2,1,0:T(8,128)(2,1)} %param.14, bf16[512,1024]{1,0:T(8,128)(2,1)} %all-gather.4.cloned.1.call-done, bf16[1,1024,512]{2,1,0:T(8,128)(2,1)} %param.13), kind=kOutput, calls=%fused_computation.39 | convolution fusion | flops 1076101120 | bytes 5242880 | tf_op jit(solution)/shard_map/dot_general | solution.py:71
  163.4 33.9 %reduce-scatter.5.cloned.1.call-done = f32[64,1024]{1,0:T(8,128)} async-done(((f32[512,1024]{1,0:T(8,128)}), f32[64,1024]{1,0:T(8,128)}) %reduce-scatter.5.cloned.1.call-update) | async-done | bytes 262160 | tf_op jit(solution)/shard_map/reduce_scatter | solution.py:72
  199.0 44.2 %all-gather.6.cloned.1.call-done = bf16[1024,1024]{1,0:T(8,128)(2,1)} async-done(((bf16[64,1024]{1,0:T(8,128)(2,1)}), bf16[1024,1024]{1,0:T(8,128)(2,1)}) %all-gather.6.cloned.1.call-update) | async-done | bytes 2097168 | tf_op jit(solution)/shard_map/all_gather | solution.py:80
  243.1 5.0 %convolution_convert_fusion.1 = bf16[512,512]{1,0:T(8,128)(2,1)} fusion(bf16[1024,512]{1,0:T(8,128)(2,1)S(1)} %copy-done.3, bf16[1024,1024]{1,0:T(8,128)(2,1)} %all-gather.6.cloned.1.call-done, f32[512,1024]{1,0:T(8,128)} %get-tuple-element.70, f32[512]{0:T(512)S(1)} %get-tuple-element.43, f32[512]{0:T(512)S(1)} %get-tuple-element.45), kind=kOutput, calls=%fused_computation.27 | convolution fusion | flops 1612972032 | bytes 5771264 | tf_op jit(solution)/shard_map/dot_general | solution.py:83
  250.6 67.9 %all-gather.8.cloned.1.call-done = bf16[8192,512]{1,0:T(8,128)(2,1)} async-done(((bf16[512,512]{1,0:T(8,128)(2,1)}), bf16[8192,512]{1,0:T(8,128)(2,1)}) %all-gather.8.cloned.1.call-update) | async-done | bytes 8388624 | tf_op jit(solution)/shard_map/all_gather | solution.py:95
  318.4 5.7 %gather_fusion = bf16[256,512]{1,0:T(8,128)(2,1)S(1)} fusion(bf16[8192,512]{1,0:T(8,128)(2,1)} %all-gather.8.cloned.1.call-done, s32[1024]{0:T(1024)S(1)} %pad_clamp_fusion), kind=kCustom, calls=%fused_computation | custom fusion | bytes 525312 | tf_op jit(solution)/shard_map/jit(_take)/gather | solution.py:96
  324.6 2.2 fusion.48
  327.9 5.3 %all-to-all-start = ((bf16[3,16,32,256]{3,2,0,1:T(8,128)(2,1)}), bf16[3,16,32,256]{3,2,0,1:T(8,128)(2,1)S(1)}, u32[]{:S(2)}, u32[]{:S(2)}) async-start(bf16[3,16,32,256]{3,2,0,1:T(8,128)(2,1)} %copy.19), calls=%async_computation.2 | async-start | bytes 1572864 | tf_op jit(solution)/shard_map/all_to_all | solution.py:106
  333.2 14.2 %all-to-all-done = bf16[3,16,32,256]{3,2,0,1:T(8,128)(2,1)S(1)} async-done(((bf16[3,16,32,256]{3,2,0,1:T(8,128)(2,1)}), bf16[3,16,32,256]{3,2,0,1:T(8,128)(2,1)S(1)}, u32[]{:S(2)}, u32[]{:S(2)}) %all-to-all-start) | async-done | bytes 786464 | tf_op jit(solution)/shard_map/all_to_all | solution.py:106
  350.6 48.1 %while.10 = (s32[]{:T(128)}, bf16[8,1,32,512]{3,2,1,0:T(8,128)(2,1)}, bf16[8,1,32,512]{3,2,1,0:T(8,128)(2,1)}, bf16[1,32,4096]{2,1,0:T(8,128)(2,1)S(1)}, bf16[1,32,4096]{2,1,0:T(8,128)(2,1)S(1)}, /*index=5*/s32[]{:T(128)}) while((s32[]{:T(128)}, bf16[8,1,32,512]{3,2,1,0:T(8,128)(2,1)}, bf16[8,1,32,512]{3,2,1,0:T(8,128)(2,1)}, ...), condition=%wide.region_15.16_spmd, body=%wide.region_12.15_spmd.sunk | while | flops 283147264 | bytes 25764932 | solution.py:41
  350.7 2.1 multiply_reduce_fusion.2
  362.7 2.1 multiply_reduce_fusion.2
  399.7 3.8 copy.25
  404.1 23.4 %reduce.6 = bf16[4096,32]{1,0:T(8,128)(2,1)S(1)} reduce(bf16[4096,1,32]{2,1,0:T(2,128)(2,1)} %bitcast.92, bf16[]{:T(256)} %broadcast.124), dimensions={1}, to_apply=%bitcast.67.reduce_sub_computation | reduce | bytes 524290
  429.2 12.0 %all_to_all.33 = bf16[16,2,4096]{2,1,0:T(2,128)(2,1)S(1)} all-to-all(bf16[16,2,4096]{2,1,0:T(2,128)(2,1)} %reshape.140), channel_id=1, replica_groups=mesh['clip'=8,'tok'=16] {'tok'}, dimensions={0} | all-to-all | bytes 524288 | tf_op jit(solution)/shard_map/all_to_all | solution.py:108
  441.2 3.6 reshape.141
  444.8 4.5 copy.26
  (80 shorter events, 63.5 us)
Async XLA Ops:
  6.5 3.2 copy-start
  6.5 3.3 copy-start.1
  6.5 128.0 %reduce-scatter.3.cloned.1.call-start = ((), (), s32[]{:S(2)}) async-start(), calls=%async_computation.4 | async-start | bytes 4456448 | tf_op jit(solution)/shard_map/reduce_scatter | solution.py:58
  59.5 0.7 copy-start.5
  59.5 99.2 %all-gather.4.cloned.1.call-start = ((), (), s32[]{:S(2)}) async-start(), calls=%async_computation.5 | async-start | bytes 1179648 | tf_op jit(solution)/shard_map/all_gather | solution.py:66
  136.3 61.0 %reduce-scatter.5.cloned.1.call-start = ((), (), s32[]{:S(2)}) async-start(), calls=%async_computation.6 | async-start | bytes 2359296 | tf_op jit(solution)/shard_map/reduce_scatter | solution.py:72
  163.3 79.8 %copy-start.3 = (bf16[1024,512]{1,0:T(8,128)(2,1)S(1)}, bf16[1024,512]{1,0:T(8,128)(2,1)}, u32[]{:S(2)}) copy-start(bf16[1024,512]{1,0:T(8,128)(2,1)} %param.15) | copy-start | bytes 3145732
  163.3 79.8 %all-gather.6.cloned.1.call-start = ((), (), s32[]{:S(2)}) async-start(), calls=%async_computation.7 | async-start | bytes 2228224 | tf_op jit(solution)/shard_map/all_gather | solution.py:80
  198.9 119.5 %all-gather.8.cloned.1.call-start = ((), (), s32[]{:S(2)}) async-start(), calls=%async_computation.8 | async-start | bytes 8912896 | tf_op jit(solution)/shard_map/all_gather | solution.py:95
  243.1 5.0 %copy-start.2 = (bf16[512]{0:T(512)(128)(2,1)S(1)}, bf16[512]{0:T(512)(128)(2,1)}, u32[]{:S(2)}) copy-start(bf16[512]{0:T(512)(128)(2,1)} %param.17) | copy-start | bytes 3076
  327.9 19.5 %all-to-all-start = ((bf16[3,16,32,256]{3,2,0,1:T(8,128)(2,1)}), bf16[3,16,32,256]{3,2,0,1:T(8,128)(2,1)S(1)}, u32[]{:S(2)}, u32[]{:S(2)}) async-start(bf16[3,16,32,256]{3,2,0,1:T(8,128)(2,1)} %copy.19), calls=%async_computation.2 | async-start | bytes 1572864 | tf_op jit(solution)/shard_map/all_to_all | solution.py:106
  441.2 8.2 %copy-start.4 = (bf16[512,512]{1,0:T(8,128)(2,1)S(1)}, bf16[512,512]{1,0:T(8,128)(2,1)}, u32[]{:S(2)}) copy-start(bf16[512,512]{1,0:T(8,128)(2,1)} %param.19) | copy-start | bytes 1572868
Sparse Core Ops, SparseCore 0:
  59.6 74.9 reduce-scatter.2
  136.4 22.2 all-gather.3
  163.5 33.7 reduce-scatter.4
  199.3 43.8 all-gather.5
  248.2 70.1 all-gather.7
where the time goes:
time: 458 us; the launch traced here: 457 us
  waiting for transfers between devices  218 us (48%)
  blocking collectives  89.8 us (20%)
  matrix products  53.5 us (12%)
  other arithmetic  50.5 us (11%)
  local copies, waits for them, and re-layouts  26.3 us (6%)
  between operations  14 us (3%)
  starting transfers between devices  5.47 us (1%)
    all_gather x1, waiting for transfers between devices, per_device(): everyone = lax.all_gather(projected, 'tok', axis=0, tiled=True)  67.9 us
    all_gather x1, waiting for transfers between devices, per_device(): lax.all_gather(slot_out, 'tok', axis=0, tiled=True)  44.2 us
    pmax x1, blocking collectives, per_device(): col_top = lax.pmax(jnp.max(logits, axis=0), 'tok')  42 us
    unnamed x1, blocking collectives  35.8 us
    reduce_scatter x1, waiting for transfers between devices, per_device(): lax.psum_scatter(slot_sums, 'tok', scatter_dimension=0, tiled=True)  35.1 us
    reduce_scatter x1, waiting for transfers between devices, per_device(): lax.psum_scatter(partial_out, 'clip', scatter_dimension=0, tiled=True)  33.9 us
    unnamed x1, other arithmetic  23.4 us
    all_gather x1, waiting for transfers between devices, per_device(): lax.all_gather(slot_in, 'clip', axis=0, tiled=True)  22.4 us
  transfers between devices with their start and end apart: 6, of which 6 were waited for; matrix products, arithmetic and copies ran while one was open for 1% of the time, Pallas kernels for 0%

commit v1 on v0

v1 whole, which is shorter than its diff:
```python
import functools
import math

import jax
import jax.numpy as jnp
import numpy as np
from jax import lax
from jax.experimental import pallas as pl
from jax.experimental.pallas import tpu as pltpu
from jax.sharding import PartitionSpec as P

MESH = pl.DeviceIdType.MESH
F32 = jnp.float32
BF16 = jnp.bfloat16
D = 1024
SL = 64
SLOTS = 1024
DD = 512
VIS = 512
POS = 256
CAP = 16
HEADS = 16
HD = 32
HID = 512
R = 4
NT = 16
NC = 8
EXT = 128
KC = 512


def dot(a, b, ca=1, cb=0):
    return lax.dot_general(a, b, (((ca,), (cb,)), ((), ())), preferred_element_type=F32)


def layer_norm(v):
    centre = v - jnp.mean(v, axis=-1, keepdims=True)
    spread = jnp.mean(centre * centre, axis=-1, keepdims=True)
    return centre * lax.rsqrt(spread + 1e-05)


def iota(shape, dim):
    return lax.broadcasted_iota(jnp.int32, shape, dim)


def kernel(
    tokens_h, keys_h, w_in_h, w_back_h, w_proj_h, src_ref, mask_ref, w_qkv_h, w_out_h, freq_ref,
    out_ref,
    tokens, keys, w_in, w_back, w_proj, w_qkv, w_out,
    normed, logits, w_bp, w_qkvt, ranks,
    send_e, recv_e, combine, filler, dec_in,
    m_send, m_recv,
    s_y, r_y, s_z, r_z, s_y2, r_y2, s_z2, r_z2,
    ag_b, part_c, recv_c, ag_d, send_f, recv_f,
    k_rows, v_ext, sc0, sc1, att, recv_g,
    load_sem, e_s, e_r, m_s, m_r, a1_s, a1_r, a2_s, a2_r, b_s, b_r, c_s, c_r, d_s, d_r, f_s, f_r, g_s, g_r,
):
    c = lax.axis_index("clip")
    t = lax.axis_index("tok")
    x, co = c // 2, lax.rem(c, 2)
    y, z = t // R, lax.rem(t, R)

    def mod(v):
        return lax.rem(v, R)

    def rc(src, dst, ss, rs, dev):
        return pltpu.make_async_remote_copy(
            src_ref=src, dst_ref=dst, send_sem=ss, recv_sem=rs, device_id=dev, device_id_type=MESH
        )

    loads = {}
    for i, (name, h, v) in enumerate(
        (
            ("tokens", tokens_h, tokens), ("keys", keys_h, keys), ("w_proj", w_proj_h, w_proj),
            ("w_back", w_back_h, w_back), ("w_in", w_in_h, w_in), ("w_qkv", w_qkv_h, w_qkv),
            ("w_out", w_out_h, w_out),
        )
    ):
        loads[name] = pltpu.make_async_copy(h, v, load_sem.at[i])
        loads[name].start()

    offsets = [(dy, dz) for dy in range(R) for dz in range(R) if dy or dz]

    def tok_at(dy, dz):
        return mod(y + dy) * R + mod(z + dz)

    def clip_at(dx, f):
        return mod(x + dx) * 2 + (co if f == 0 else 1 - co)

    clip_offsets = [(0, 1)] + [(dx, f) for dx in (1, 3, 2) for f in (0, 1)]

    barrier = pltpu.get_barrier_semaphore()
    for dy, dz in offsets:
        pl.semaphore_signal(barrier, inc=1, device_id=(c, tok_at(dy, dz)), device_id_type=MESH)
    for dx, f in clip_offsets:
        pl.semaphore_signal(barrier, inc=1, device_id=(clip_at(dx, f), t), device_id_type=MESH)

    loads["tokens"].wait()
    for r in range(0, VIS, 128):
        normed[r : r + 128, 0:D] = layer_norm(tokens[r : r + 128, :].astype(F32)).astype(BF16)
    normed[:, D:] = jnp.ones((VIS, EXT), BF16)
    loads["keys"].wait()
    tops = []
    for k in range(4):
        part = dot(normed[:, 0:D], keys[:, k * 256 : (k + 1) * 256])
        logits[:, k * 256 : (k + 1) * 256] = part
        tops.append(jnp.max(part, axis=0, keepdims=True))
    for k in range(4):
        m_send[2 * k : 2 * k + 1, :] = tops[k][:, 0:128]
        m_send[2 * k + 1 : 2 * k + 2, :] = tops[k][:, 128:256]

    pl.semaphore_wait(barrier, len(offsets) + len(clip_offsets))
    m_cp = [
        rc(m_send, m_recv.at[i], m_s.at[i], m_r.at[i], (c, tok_at(dy, dz)))
        for i, (dy, dz) in enumerate(offsets)
    ]
    for cp in m_cp:
        cp.start()

    col = iota((1, POS), 1)
    for b in range(NT):
        mine = src_ref[:, b * POS : (b + 1) * POS]
        ranks[b : b + 1, :] = (lax.shift_right_logical(mine, 9) == t).astype(F32)
    before = (iota((POS, POS), 0) < iota((POS, POS), 1)).astype(F32).astype(BF16)
    ranks[NT:, :] = dot(ranks[0:NT, :].astype(BF16), before)
    for b in range(NT):
        mine = src_ref[:, b * POS : (b + 1) * POS]
        here = lax.shift_right_logical(mine, 9) == t
        code = jnp.where(here, ranks[NT + b : NT + b + 1, :].astype(jnp.int32), CAP)
        local = (mine & (VIS - 1)).astype(F32) + 1.0
        pick = jnp.where(code == iota((CAP, POS), 0), local, 0.0)
        row = jnp.sum(pick, axis=1, keepdims=True)
        onehot = (row == (iota((CAP, VIS), 1) + 1).astype(F32)).astype(F32).astype(BF16)
        send_e[b, :, 0:VIS] = onehot
    hot = send_e[:, :, 0:VIS].reshape(NT * CAP, VIS)
    rows = dot(hot, normed[:, 0:D]).astype(BF16)
    send_e[...] = rows.reshape(NT, CAP, D)
    recv_e[pl.ds(t, 1)] = send_e[pl.ds(t, 1)]
    e_cp = [
        rc(send_e.at[tok_at(dy, dz)], recv_e.at[t], e_s.at[i], e_r.at[i], (c, tok_at(dy, dz)))
        for i, (dy, dz) in enumerate(offsets)
    ]
    for cp in e_cp:
        cp.start()

    top8 = m_send[...]
    for i, cp in enumerate(m_cp):
        cp.wait_recv()
    for i in range(len(m_cp)):
        top8 = jnp.maximum(top8, m_recv[i])
    m_send_done = m_cp
    for cp in m_send_done:
        cp.wait_send()
    m_send[...] = top8

    y1, z1 = [], []
    for d in (1, 3, 2, 0):
        yy = mod(y + d)
        lanes = pl.ds(pl.multiple_of(yy * 256, 256), 256)
        pair = m_send[pl.ds(yy * 2, 2), :]
        top = jnp.concatenate([pair[0:1, :], pair[1:2, :]], axis=1)
        disp = jnp.exp(logits[:, lanes] - top).astype(BF16)
        sums = dot(disp, normed[...], 0, 0)
        s_y[pl.ds(yy, 1), :, 0:512] = sums[:, 0:512].astype(BF16)[None]
        s_y[pl.ds(yy, 1), :, 512:] = sums[:, D:].astype(BF16)[None]
        s_z[pl.ds(yy, 1)] = sums[:, 512:D].astype(BF16).reshape(1, R, SL, 512)
        if d:
            cp = rc(s_y.at[yy], r_y.at[d - 1], a1_s.at[d - 1], a1_r.at[d - 1], (c, tok_at(d, 0)))
            cp.start()
            y1.append(cp)
    for d in (1, 3, 2):
        zz = mod(z + d)
        cp = rc(s_z.at[:, zz], r_z.at[d - 1], a1_s.at[2 + d], a1_r.at[2 + d], (c, tok_at(0, d)))
        cp.start()
        z1.append(cp)

    loads["w_proj"].wait()
    loads["w_back"].wait()
    w_bp[...] = dot(w_back[...], w_proj[...]).astype(BF16)
    loads["w_qkv"].wait()
    for k in range(3):
        w_qkvt[k * DD : (k + 1) * DD, :] = w_qkv[:, k * DD : (k + 1) * DD].T
    place = (iota((POS, 1), 0) + t * POS).astype(F32)
    angle = place * freq_ref[...]
    mask = mask_ref[...].astype(F32)
    filler[:, 0:256] = (mask[:, 0:256] + jnp.sin(angle)).astype(BF16)
    filler[:, 256:512] = (mask[:, 256:512] + jnp.cos(angle)).astype(BF16)

    for cp in y1:
        cp.wait_recv()
    y2, own_y = [], None
    for d in (1, 3, 2, 0):
        at = pl.ds(pl.multiple_of(mod(z + d) * SL, SL), SL)
        total = s_y[pl.ds(y, 1), at, :].astype(F32)[0]
        for i in range(3):
            total = total + r_y[i, at, :].astype(F32)
        if d:
            s_y2[d - 1] = total.astype(BF16)
            cp = rc(s_y2.at[d - 1], r_y2.at[d - 1], a2_s.at[d - 1], a2_r.at[d - 1], (c, tok_at(0, d)))
            cp.start()
            y2.append(cp)
        else:
            own_y = total
    for cp in z1:
        cp.wait_recv()
    z2, own_z = [], None
    for d in (1, 3, 2, 0):
        yy = mod(y + d)
        total = s_z[pl.ds(yy, 1), pl.ds(z, 1)].astype(F32)[0, 0]
        for i in range(3):
            total = total + r_z[i, pl.ds(yy, 1)].astype(F32)[0]
        if d:
            s_z2[d - 1] = total.astype(BF16)
            cp = rc(s_z2.at[d - 1], r_z2.at[d - 1], a2_s.at[2 + d], a2_r.at[2 + d], (c, tok_at(d, 0)))
            cp.start()
            z2.append(cp)
        else:
            own_z = total

    for cp in e_cp:
        cp.wait_recv()
    got = recv_e[...].reshape(NT * CAP, D)
    lg = dot(got, keys[...])
    raised = jnp.exp(lg - jnp.max(lg, axis=1, keepdims=True))
    comb = (raised / jnp.sum(raised, axis=1, keepdims=True)).astype(BF16)
    own_row = src_ref[:, pl.ds(pl.multiple_of(t * POS, POS), POS)]
    block_row = lax.shift_right_logical(own_row, 9)
    square0, square1 = iota((POS, POS), 0), iota((POS, POS), 1)
    block_col = jnp.sum(
        jnp.where(square0 == square1, block_row.astype(F32), 0.0), axis=1, keepdims=True
    )
    same = (block_col == block_row.astype(F32)) & (square1 < square0)
    rank_col = jnp.sum(jnp.where(same, 1.0, 0.0), axis=1, keepdims=True)
    target = block_col * CAP + rank_col
    target = jnp.where(block_col >= NT, -1.0, target)
    place_hot = (target == square1.astype(F32)).astype(F32).astype(BF16)
    combine[...] = dot(place_hot, comb).astype(BF16)

    for cp in y2 + z2:
        cp.wait_recv()
    for i in range(3):
        own_y = own_y + r_y2[i].astype(F32)
        own_z = own_z + r_z2[i].astype(F32)
    inverse = 1.0 / own_y[:, 512:513]
    ag_b[pl.ds(c, 1), :, 0:512] = (own_y[:, 0:512] * inverse).astype(BF16)[None]
    ag_b[pl.ds(c, 1), :, 512:] = (own_z * inverse).astype(BF16)[None]

    b_cp = {}
    for dx in (1, 3, 2):
        b_cp[dx] = rc(ag_b.at[c], ag_b.at[c], b_s.at[dx - 1], b_r.at[dx - 1], (clip_at(dx, 0), t))
        b_cp[dx].start()
    partner = (clip_at(0, 1), t)
    fw = {0: rc(ag_b.at[c], ag_b.at[c], b_s.at[3], b_r.at[3], partner)}
    fw[0].start()
    loads["w_in"].wait()
    c_cp = []
    for step, dx in enumerate((0, 1, 3, 2)):
        chip = mod(x + R - dx)
        if dx:
            b_cp[dx].wait_recv()
            held = ag_b.at[chip * 2 + co]
            fw[dx] = rc(held, held, b_s.at[3 + dx], b_r.at[3 + dx], partner)
            fw[dx].start()
        fw[dx].wait_recv()
        rows = ag_b[pl.ds(chip * 2, 2)].reshape(2 * SL, D)
        hidden = jax.nn.gelu(dot(rows, w_in[...])).astype(BF16)
        part_c[pl.ds(chip * 2, 2)] = dot(hidden, w_bp[...]).astype(BF16).reshape(2, SL, DD)
        for f in (0, 1):
            if dx == 0 and f == 0:
                continue
            i = ((R - dx) % R) * 2 + f - 1
            to = clip_at(R - dx, f)
            cp = rc(part_c.at[to], recv_c.at[i], c_s.at[i], c_r.at[i], (to, t))
            cp.start()
            c_cp.append(cp)

    for cp in c_cp:
        cp.wait_recv()
    total = part_c[pl.ds(c, 1)].astype(F32)[0]
    for i in range(NC - 1):
        total = total + recv_c[i].astype(F32)
    ag_d[pl.ds(y, 1), pl.ds(z, 1)] = total.astype(BF16).reshape(1, 1, SL, DD)

    lo, hi = pl.ds(0, 256), pl.ds(256, 256)
    d1y, d1z, d2 = {}, {}, []
    for d in (1, 3, 2):
        d1y[d] = rc(
            ag_d.at[y, z, :, lo], ag_d.at[y, z, :, lo], d_s.at[d - 1], d_r.at[d - 1], (c, tok_at(d, 0))
        )
        d1y[d].start()
        d1z[d] = rc(
            ag_d.at[y, z, :, hi], ag_d.at[y, z, :, hi], d_s.at[2 + d], d_r.at[2 + d], (c, tok_at(0, d))
        )
        d1z[d].start()
    for d in (0, 1, 3, 2):
        if d:
            d1y[d].wait_recv()
            d1z[d].wait_recv()
        ya, za = mod(y + R - d), mod(z + R - d)
        for e in (1, 3, 2):
            i = 6 + d * 6 + (e - 1) * 2
            cp = rc(ag_d.at[ya, z, :, lo], ag_d.at[ya, z, :, lo], d_s.at[i], d_r.at[i], (c, tok_at(0, e)))
            cp.start()
            d2.append(cp)
            cp = rc(
                ag_d.at[y, za, :, hi], ag_d.at[y, za, :, hi], d_s.at[i + 1], d_r.at[i + 1], (c, tok_at(e, 0))
            )
            cp.start()
            d2.append(cp)
    for cp in d2:
        cp.wait_recv()

    shown = dot(combine[...], ag_d[...].reshape(SLOTS, DD)).astype(BF16)
    visible = block_col < NT
    held = jnp.where(visible, shown.astype(F32), filler[...].astype(F32))
    dec_in[...] = held.astype(BF16)
    dec_normed = layer_norm(held).astype(BF16)
    scale = math.log2(math.e) / math.sqrt(HD)
    for k in range(3):
        part = dot(w_qkvt[k * DD : (k + 1) * DD, :], dec_normed, 1, 1)
        if k == 0:
            part = part * scale
        send_f[:, k * HD : (k + 1) * HD, :] = part.astype(BF16).reshape(HEADS, HD, POS)
    recv_f[pl.ds(t, 1)] = send_f[pl.ds(t, 1)]
    f_cp = [
        rc(send_f.at[tok_at(dy, dz)], recv_f.at[t], f_s.at[i], f_r.at[i], (c, tok_at(dy, dz)))
        for i, (dy, dz) in enumerate(offsets)
    ]
    for cp in f_cp:
        cp.start()
    v_ext[HD:, :] = jnp.where(iota((16, NT * POS), 0) == 0, 1.0, 0.0).astype(BF16)
    for cp in f_cp:
        cp.wait_recv()

    def gather_keys(s, _):
        at = pl.ds(pl.multiple_of(s * POS, POS), POS)
        k_rows[at, :] = recv_f[s, HD : 2 * HD, :].T
        v_ext[0:HD, at] = recv_f[s, 2 * HD :, :]
        return 0

    lax.fori_loop(0, NT, gather_keys, 0)

    def scores(block, into):
        q = recv_f[block, 0:HD, :]
        top = None
        for k in range(NT * POS // KC):
            s = dot(k_rows[k * KC : (k + 1) * KC, :], q)
            into[k * KC : (k + 1) * KC, :] = s
            m = jnp.max(s.reshape(KC // 8, 8, POS), axis=0)
            top = m if top is None else jnp.maximum(top, m)
        return jnp.max(top, axis=0, keepdims=True)

    def finish(block, held, top):
        acc = jnp.zeros((HD + 16, POS), F32)
        for k in range(NT * POS // KC):
            p = jnp.exp2(held[k * KC : (k + 1) * KC, :] - top).astype(BF16)
            acc = acc + dot(v_ext[:, k * KC : (k + 1) * KC], p)
        att[pl.ds(block, 1)] = (acc[0:HD] / acc[HD : HD + 1]).astype(BF16)[None]

    def g_copy(i, block):
        return rc(att.at[block], recv_g.at[t], g_s.at[i], g_r.at[i], (c, block))

    def send_block(i, block):
        @pl.when(i < NT - 1)
        def _():
            g_copy(i, block).start()

    def at_step(i):
        return lax.rem(t + 1 + i, NT)

    top0 = scores(at_step(0), sc0)

    def two(j, top0):
        i = 2 * j
        top1 = scores(at_step(i + 1), sc1)
        finish(at_step(i), sc0, top0)
        send_block(i, at_step(i))
        nxt = scores(at_step(lax.rem(i + 2, NT)), sc0)
        finish(at_step(i + 1), sc1, top1)
        send_block(i + 1, at_step(i + 1))
        return nxt

    lax.fori_loop(0, NT // 2, two, top0)
    recv_g[pl.ds(t, 1)] = att[pl.ds(t, 1)]
    loads["w_out"].wait()
    for i in range(NT - 1):
        g_copy(i, at_step(i)).wait_recv()
    mixed = dot(recv_g[...].reshape(DD, POS), w_out[...], 0, 0)
    out_ref[...] = (mixed + dec_in[...].astype(F32)).astype(BF16)

    for cp in e_cp + y1 + z1 + y2 + z2 + list(b_cp.values()) + list(fw.values()) + c_cp:
        cp.wait_send()
    for cp in list(d1y.values()) + list(d1z.values()) + d2 + f_cp:
        cp.wait_send()
    for i in range(NT - 1):
        g_copy(i, at_step(i)).wait_send()


def per_device(tokens, slot_keys, w_in, w_back, w_proj, dec_source, mask_token, w_qkv, w_out):
    freq = jnp.asarray(np.exp(-math.log(10000.0) * np.arange(DD // 2) / (DD // 2)).astype(np.float32))
    V = pltpu.VMEM
    dma = lambda n: pltpu.SemaphoreType.DMA((n,))
    hbm = pl.BlockSpec(memory_space=pl.ANY)
    vm = pl.BlockSpec(memory_space=pltpu.VMEM)
    return pl.pallas_call(
        kernel,
        out_shape=jax.ShapeDtypeStruct((POS, DD), BF16),
        in_specs=[hbm, hbm, hbm, hbm, hbm, vm, vm, hbm, hbm, vm],
        out_specs=vm,
        scratch_shapes=[
            V((VIS, D), BF16), V((D, SLOTS), BF16), V((D, HID), BF16), V((HID, D), BF16),
            V((D, DD), BF16), V((DD, 3 * DD), BF16), V((DD, DD), BF16),
            V((VIS, D + EXT), BF16), V((VIS, SLOTS), F32), V((HID, DD), BF16), V((3 * DD, DD), BF16),
            V((2 * NT, POS), F32),
            V((NT, CAP, D), BF16), V((NT, CAP, D), BF16), V((POS, SLOTS), BF16), V((POS, DD), BF16),
            V((POS, DD), BF16),
            V((8, 128), F32), V((NT - 1, 8, 128), F32),
            V((R, 256, 512 + EXT), BF16), V((3, 256, 512 + EXT), BF16),
            V((R, R, SL, 512), BF16), V((3, R, SL, 512), BF16),
            V((3, SL, 512 + EXT), BF16), V((3, SL, 512 + EXT), BF16),
            V((3, SL, 512), BF16), V((3, SL, 512), BF16),
            V((NC, SL, D), BF16), V((NC, SL, DD), BF16), V((NC - 1, SL, DD), BF16),
            V((R, R, SL, DD), BF16), V((HEADS, 3 * HD, POS), BF16), V((NT, 3 * HD, POS), BF16),
            V((NT * POS, HD), BF16), V((HD + 16, NT * POS), BF16),
            V((NT * POS, POS), F32), V((NT * POS, POS), F32),
            V((NT, HD, POS), BF16), V((HEADS, HD, POS), BF16),
            dma(7), dma(15), dma(15), dma(15), dma(15), dma(6), dma(6), dma(6), dma(6),
            dma(7), dma(7), dma(7), dma(7), dma(30), dma(30), dma(15), dma(15), dma(15), dma(15),
        ],
        compiler_params=pltpu.CompilerParams(
            collective_id=0, has_side_effects=True, vmem_limit_bytes=60 << 20
        ),
        name="moe_mae",
    )(
        tokens, slot_keys, w_in[0], w_back[0], w_proj, dec_source, mask_token[None], w_qkv, w_out, freq[None]
    )


def solution(mesh):
    placed = (
        P(("clip", "tok"), None),
        P(),
        P("tok", None, "clip"),
        P("tok", "clip", None),
        P(),
        P("clip", None),
        P(),
        P(),
        P(),
    )
    return jax.shard_map(
        per_device, mesh=mesh, in_specs=placed, out_specs=P(("clip", "tok"), None), check_vma=False
    )
```

time: 458 us -> 102 us (0.22)
  waiting for transfers between devices: 218 us -> 0 us
  Pallas kernels: 0 us -> 99 us
  blocking collectives: 89.8 us -> 0 us
  matrix products: 53.5 us -> 0 us
  other arithmetic: 50.5 us -> 0 us
  local copies, waits for them, and re-layouts: 26.3 us -> 2.93 us
  between operations: 14 us -> 0.01 us
  starting transfers between devices: 5.47 us -> 0 us
    all_gather x3 -> x0, waiting for transfers between devices: 134 us -> none  [the longest x1 67.9 us: per_device(): everyone = lax.all_gather(projected, 'tok', axis=0, tiled=True)]
    pallas_call x0 -> x1, Pallas kernels: none -> 99 us  [per_device(): pl.pallas_call(kernel, out_shape=jax.ShapeDtypeStruct((POS, DD), BF16), i...]
    reduce_scatter x2 -> x0, waiting for transfers between devices: 68.9 us -> none  [the longest x1 35.1 us: per_device(): lax.psum_scatter(slot_sums, 'tok', scatter_dimension=0, tiled=True)]
    dot_general x21 -> x0, matrix products: 51.2 us -> none  [the longest x8 16.9 us: one_block(): jnp.einsum('hkq,hkn->hqn', query_block, key_rows, preferred_element_type=...]
    pmax x1 -> x0, blocking collectives: 42 us -> none  [per_device(): col_top = lax.pmax(jnp.max(logits, axis=0), 'tok')]
    unnamed x1 -> x0, blocking collectives: 35.8 us -> none
    unnamed x1 -> x0, other arithmetic: 23.4 us -> none
    reduce_sum x13 -> x0, other arithmetic: 21.2 us -> none  [the longest x8 15.2 us: one_block(): totals = jnp.sum(raised.astype(jnp.float32), axis=-1)]
  transfers between devices with their start and end apart: 6 -> 0, of which waited for: 6 -> 0; matrix products, arithmetic and copies ran while one was open for 1% -> 0% of each run, Pallas kernels for 0% -> 0%
where the time goes in v1:
time: 102 us
  Pallas kernels  99 us (97%)
  local copies, waits for them, and re-layouts  2.93 us (3%)
    pallas_call x1, Pallas kernels, per_device(): pl.pallas_call(kernel, out_shape=jax.ShapeDtypeStruct((POS, DD), BF16), i...  99 us

profile of v1, /device:TPU:0, one launch (start us, length us, event | category | flops | bytes accessed | tf_op | source)
XLA Modules:
  0.0 101.9 jit_solution(449858073712227998)
XLA Ops:
  0.0 1.3 %broadcast_in_dim.6.mask_ref = bf16[1,512]{1,0:T(2,128)(2,1)} reshape(bf16[512]{0:T(512)(128)(2,1)} %param.16) | data formatting | bytes 2048 | tf_op jit(solution)/shard_map/broadcast_in_dim | solution.py:435
  1.3 99.0 %moe_mae.1 = bf16[256,512]{1,0:T(8,128)(2,1)} custom-call(bf16[512,1024]{1,0:T(8,128)(2,1)} %tokens_h.1, bf16[1024,1024]{1,0:T(8,128)(2,1)} %keys_h.1, bf16[1024,512]{1,0:T(8,128)(2,1)} %bitcast.2, bf16[512,1024]{1,0:T(8,128)(2,1)} %bitcast.3, bf16[1024,512]{1,0:T(8,128)(2,1)} %w_proj_h.1, s32[1,4096]{1,0:T(1,128)} %src_ref.1, ...), custom_call_target="tpu_custom_call" | custom-call | tf_op jit(solution)/shard_map/moe_mae/pallas_call | solution.py:405
  100.3 1.7 %copy.12 = bf16[256,512]{1,0:T(8,128)(2,1)} copy(bf16[256,512]{1,0:T(8,128)(2,1)} %moe_mae.1) | data formatting | bytes 524288

commit v2 on v1

--- a/solution.py
+++ b/solution.py
@@ -53,7 +53,7 @@
     s_y, r_y, s_z, r_z, s_y2, r_y2, s_z2, r_z2,
     ag_b, part_c, recv_c, ag_d, send_f, recv_f,
     k_rows, v_ext, sc0, sc1, att, recv_g,
-    load_sem, e_s, e_r, m_s, m_r, a1_s, a1_r, a2_s, a2_r, b_s, b_r, c_s, c_r, d_s, d_r, f_s, f_r, g_s, g_r,
+    load_sem, e_s, e_r, m_s, m_r, a1_s, a1_r, a2_s, a2_r, b_s, b_r, c_s, c_r, d_s, d_r, f_s, f_r, g_s, g_r, q_s, q_r,
 ):
     c = lax.axis_index("clip")
     t = lax.axis_index("tok")
@@ -140,8 +140,6 @@
         rc(send_e.at[tok_at(dy, dz)], recv_e.at[t], e_s.at[i], e_r.at[i], (c, tok_at(dy, dz)))
         for i, (dy, dz) in enumerate(offsets)
     ]
-    for cp in e_cp:
-        cp.start()
 
     top8 = m_send[...]
     for i, cp in enumerate(m_cp):
@@ -182,7 +180,7 @@
         w_qkvt[k * DD : (k + 1) * DD, :] = w_qkv[:, k * DD : (k + 1) * DD].T
     place = (iota((POS, 1), 0) + t * POS).astype(F32)
     angle = place * freq_ref[...]
-    mask = mask_ref[...].astype(F32)
+    mask = mask_ref[...].astype(F32).reshape(1, DD)
     filler[:, 0:256] = (mask[:, 0:256] + jnp.sin(angle)).astype(BF16)
     filler[:, 256:512] = (mask[:, 256:512] + jnp.cos(angle)).astype(BF16)
 
@@ -217,27 +215,10 @@
         else:
             own_z = total
 
+    for cp in y2 + z2:
+        cp.wait_recv()
     for cp in e_cp:
-        cp.wait_recv()
-    got = recv_e[...].reshape(NT * CAP, D)
-    lg = dot(got, keys[...])
-    raised = jnp.exp(lg - jnp.max(lg, axis=1, keepdims=True))
-    comb = (raised / jnp.sum(raised, axis=1, keepdims=True)).astype(BF16)
-    own_row = src_ref[:, pl.ds(pl.multiple_of(t * POS, POS), POS)]
-    block_row = lax.shift_right_logical(own_row, 9)
-    square0, square1 = iota((POS, POS), 0), iota((POS, POS), 1)
-    block_col = jnp.sum(
-        jnp.where(square0 == square1, block_row.astype(F32), 0.0), axis=1, keepdims=True
-    )
-    same = (block_col == block_row.astype(F32)) & (square1 < square0)
-    rank_col = jnp.sum(jnp.where(same, 1.0, 0.0), axis=1, keepdims=True)
-    target = block_col * CAP + rank_col
-    target = jnp.where(block_col >= NT, -1.0, target)
-    place_hot = (target == square1.astype(F32)).astype(F32).astype(BF16)
-    combine[...] = dot(place_hot, comb).astype(BF16)
-
-    for cp in y2 + z2:
-        cp.wait_recv()
+        cp.start()
     for i in range(3):
         own_y = own_y + r_y2[i].astype(F32)
         own_z = own_z + r_z2[i].astype(F32)
@@ -274,6 +255,25 @@
             cp.start()
             c_cp.append(cp)
 
+    for cp in e_cp:
+        cp.wait_recv()
+    got = recv_e[...].reshape(NT * CAP, D)
+    lg = dot(got, keys[...])
+    raised = jnp.exp(lg - jnp.max(lg, axis=1, keepdims=True))
+    comb = (raised / jnp.sum(raised, axis=1, keepdims=True)).astype(BF16)
+    own_row = src_ref[:, pl.ds(pl.multiple_of(t * POS, POS), POS)]
+    block_row = lax.shift_right_logical(own_row, 9)
+    square0, square1 = iota((POS, POS), 0), iota((POS, POS), 1)
+    block_col = jnp.sum(
+        jnp.where(square0 == square1, block_row.astype(F32), 0.0), axis=1, keepdims=True
+    )
+    same = (block_col == block_row.astype(F32)) & (square1 < square0)
+    rank_col = jnp.sum(jnp.where(same, 1.0, 0.0), axis=1, keepdims=True)
+    target = block_col * CAP + rank_col
+    target = jnp.where(block_col >= NT, -1.0, target)
+    place_hot = (target == square1.astype(F32)).astype(F32).astype(BF16)
+    combine[...] = dot(place_hot, comb).astype(BF16)
+
     for cp in c_cp:
         cp.wait_recv()
     total = part_c[pl.ds(c, 1)].astype(F32)[0]
@@ -323,11 +323,23 @@
         send_f[:, k * HD : (k + 1) * HD, :] = part.astype(BF16).reshape(HEADS, HD, POS)
     recv_f[pl.ds(t, 1)] = send_f[pl.ds(t, 1)]
     f_cp = [
-        rc(send_f.at[tok_at(dy, dz)], recv_f.at[t], f_s.at[i], f_r.at[i], (c, tok_at(dy, dz)))
+        rc(
+            send_f.at[tok_at(dy, dz), HD:], recv_f.at[t, HD:], f_s.at[i], f_r.at[i], (c, tok_at(dy, dz))
+        )
         for i, (dy, dz) in enumerate(offsets)
     ]
     for cp in f_cp:
         cp.start()
+
+    def at_step(i):
+        return lax.rem(t + 1 + i, NT)
+
+    def q_copy(i):
+        to = lax.rem(t + NT - 1 - i, NT)
+        return rc(send_f.at[to, 0:HD], recv_f.at[t, 0:HD], q_s.at[i], q_r.at[i], (c, to))
+
+    for i in range(NT - 1):
+        q_copy(i).start()
     v_ext[HD:, :] = jnp.where(iota((16, NT * POS), 0) == 0, 1.0, 0.0).astype(BF16)
     for cp in f_cp:
         cp.wait_recv()
@@ -365,16 +377,21 @@
         def _():
             g_copy(i, block).start()
 
-    def at_step(i):
-        return lax.rem(t + 1 + i, NT)
-
+    def await_q(i):
+        @pl.when(i < NT - 1)
+        def _():
+            q_copy(i).wait_recv()
+
+    await_q(0)
     top0 = scores(at_step(0), sc0)
 
     def two(j, top0):
         i = 2 * j
+        await_q(i + 1)
         top1 = scores(at_step(i + 1), sc1)
         finish(at_step(i), sc0, top0)
         send_block(i, at_step(i))
+        await_q(i + 2)
         nxt = scores(at_step(lax.rem(i + 2, NT)), sc0)
         finish(at_step(i + 1), sc1, top1)
         send_block(i + 1, at_step(i + 1))
@@ -394,6 +411,7 @@
         cp.wait_send()
     for i in range(NT - 1):
         g_copy(i, at_step(i)).wait_send()
+        q_copy(i).wait_send()
 
 
 def per_device(tokens, slot_keys, w_in, w_back, w_proj, dec_source, mask_token, w_qkv, w_out):
@@ -425,14 +443,14 @@
             V((NT * POS, POS), F32), V((NT * POS, POS), F32),
             V((NT, HD, POS), BF16), V((HEADS, HD, POS), BF16),
             dma(7), dma(15), dma(15), dma(15), dma(15), dma(6), dma(6), dma(6), dma(6),
-            dma(7), dma(7), dma(7), dma(7), dma(30), dma(30), dma(15), dma(15), dma(15), dma(15),
+            dma(7), dma(7), dma(7), dma(7), dma(30), dma(30), dma(15), dma(15), dma(15), dma(15), dma(15), dma(15),
         ],
         compiler_params=pltpu.CompilerParams(
             collective_id=0, has_side_effects=True, vmem_limit_bytes=60 << 20
         ),
         name="moe_mae",
     )(
-        tokens, slot_keys, w_in[0], w_back[0], w_proj, dec_source, mask_token[None], w_qkv, w_out, freq[None]
+        tokens, slot_keys, w_in[0], w_back[0], w_proj, dec_source, mask_token, w_qkv, w_out, freq[None]
     )
 
 

time: 102 us -> 96.4 us (0.945)
  Pallas kernels: 99 us -> 94.5 us
  local copies, waits for them, and re-layouts: 2.93 us -> 1.67 us
    pallas_call x1, Pallas kernels: 99 us -> 94.5 us  [per_device(): pl.pallas_call(kernel, out_shape=jax.ShapeDtypeStruct((POS, DD), BF16), i...]
    broadcast_in_dim x1 -> x0, local copies, waits for them, and re-layouts: 1.26 us -> none  [per_device(): mask_token[None]]
where the time goes in v2:
time: 96.4 us; the launch traced here: 96.2 us
  Pallas kernels  94.5 us (98%)
  local copies, waits for them, and re-layouts  1.67 us (2%)
    pallas_call x1, Pallas kernels, per_device(): pl.pallas_call(kernel, out_shape=jax.ShapeDtypeStruct((POS, DD), BF16), i...  94.5 us

profile of v2, /device:TPU:0, one launch (start us, length us, event | category | flops | bytes accessed | tf_op | source)
XLA Modules:
  0.0 96.2 jit_solution(18050046026101768342)
XLA Ops:
  0.0 94.5 %moe_mae.1 = bf16[256,512]{1,0:T(8,128)(2,1)} custom-call(bf16[512,1024]{1,0:T(8,128)(2,1)} %tokens_h.1, bf16[1024,1024]{1,0:T(8,128)(2,1)} %keys_h.1, bf16[1024,512]{1,0:T(8,128)(2,1)} %bitcast.2, bf16[512,1024]{1,0:T(8,128)(2,1)} %bitcast.3, bf16[1024,512]{1,0:T(8,128)(2,1)} %w_proj_h.1, s32[1,4096]{1,0:T(1,128)} %src_ref.1, bf16[512]{0:T(512)(128)(2,1)} %mask_ref.1, ...), custom_call_target="tpu_custom_call" | custom-call | tf_op jit(solution)/shard_map/moe_mae/pallas_call | solution.py:423
  94.5 1.7 %copy.12 = bf16[256,512]{1,0:T(8,128)(2,1)} copy(bf16[256,512]{1,0:T(8,128)(2,1)} %moe_mae.1) | data formatting | bytes 524288

commit v3 on v2

--- a/solution.py
+++ b/solution.py
@@ -25,7 +25,7 @@
 R = 4
 NT = 16
 NC = 8
-EXT = 128
+KS = 512
 KC = 512
 
 
@@ -47,9 +47,9 @@
     tokens_h, keys_h, w_in_h, w_back_h, w_proj_h, src_ref, mask_ref, w_qkv_h, w_out_h, freq_ref,
     out_ref,
     tokens, keys, w_in, w_back, w_proj, w_qkv, w_out,
-    normed, logits, w_bp, w_qkvt, ranks,
+    normed, disp, w_bp, w_qkvt, ranks,
     send_e, recv_e, combine, filler, dec_in,
-    m_send, m_recv,
+    tops, weight,
     s_y, r_y, s_z, r_z, s_y2, r_y2, s_z2, r_z2,
     ag_b, part_c, recv_c, ag_d, send_f, recv_f,
     k_rows, v_ext, sc0, sc1, att, recv_g,
@@ -69,14 +69,13 @@
         )
 
     loads = {}
-    for i, (name, h, v) in enumerate(
-        (
-            ("tokens", tokens_h, tokens), ("keys", keys_h, keys), ("w_proj", w_proj_h, w_proj),
-            ("w_back", w_back_h, w_back), ("w_in", w_in_h, w_in), ("w_qkv", w_qkv_h, w_qkv),
-            ("w_out", w_out_h, w_out),
-        )
-    ):
-        loads[name] = pltpu.make_async_copy(h, v, load_sem.at[i])
+    wanted = [(f"tokens{k}", tokens_h, tokens, (slice(k * 128, (k + 1) * 128),)) for k in range(4)]
+    wanted += [
+        ("keys", keys_h, keys, ()), ("w_proj", w_proj_h, w_proj, ()), ("w_back", w_back_h, w_back, ()), ("w_in", w_in_h, w_in, ()),
+        ("w_qkv", w_qkv_h, w_qkv, ()), ("w_out", w_out_h, w_out, ()),
+    ]
+    for i, (name, h, v, at) in enumerate(wanted):
+        loads[name] = pltpu.make_async_copy(h.at[at] if at else h, v.at[at] if at else v, load_sem.at[i])
         loads[name].start()
 
     offsets = [(dy, dz) for dy in range(R) for dz in range(R) if dy or dz]
@@ -95,27 +94,43 @@
     for dx, f in clip_offsets:
         pl.semaphore_signal(barrier, inc=1, device_id=(clip_at(dx, f), t), device_id_type=MESH)
 
-    loads["tokens"].wait()
-    for r in range(0, VIS, 128):
-        normed[r : r + 128, 0:D] = layer_norm(tokens[r : r + 128, :].astype(F32)).astype(BF16)
-    normed[:, D:] = jnp.ones((VIS, EXT), BF16)
+    for k in range(4):
+        loads[f"tokens{k}"].wait()
+        at = slice(k * 128, (k + 1) * 128)
+        normed[at, :] = layer_norm(tokens[at, :].astype(F32)).astype(BF16)
     loads["keys"].wait()
-    tops = []
     for k in range(4):
-        part = dot(normed[:, 0:D], keys[:, k * 256 : (k + 1) * 256])
-        logits[:, k * 256 : (k + 1) * 256] = part
-        tops.append(jnp.max(part, axis=0, keepdims=True))
-    for k in range(4):
-        m_send[2 * k : 2 * k + 1, :] = tops[k][:, 0:128]
-        m_send[2 * k + 1 : 2 * k + 2, :] = tops[k][:, 128:256]
+        at = slice(k * 256, (k + 1) * 256)
+        part = dot(normed[...], keys[:, at])
+        top = jnp.max(part, axis=0, keepdims=True)
+        raised = jnp.exp(part - top).astype(BF16)
+        disp[:, at] = raised
+        tops[0, 0:1, at] = top
+        tops[0, 1:2, at] = jnp.sum(raised.astype(F32), axis=0, keepdims=True)
 
     pl.semaphore_wait(barrier, len(offsets) + len(clip_offsets))
     m_cp = [
-        rc(m_send, m_recv.at[i], m_s.at[i], m_r.at[i], (c, tok_at(dy, dz)))
+        rc(tops.at[0], tops.at[i + 1], m_s.at[i], m_r.at[i], (c, tok_at(dy, dz)))
         for i, (dy, dz) in enumerate(offsets)
     ]
     for cp in m_cp:
         cp.start()
+
+    y1, z1 = [], []
+    for d in (1, 3, 2, 0):
+        yy = mod(y + d)
+        sums = dot(disp[:, pl.ds(pl.multiple_of(yy * 256, 256), 256)], normed[...], 0, 0)
+        s_y[pl.ds(yy, 1)] = sums[:, 0:512].astype(BF16)[None]
+        s_z[pl.ds(yy, 1)] = sums[:, 512:D].astype(BF16).reshape(1, R, SL, 512)
+        if d:
+            cp = rc(s_y.at[yy], r_y.at[d - 1], a1_s.at[d - 1], a1_r.at[d - 1], (c, tok_at(d, 0)))
+            cp.start()
+            y1.append(cp)
+    for d in (1, 3, 2):
+        zz = mod(z + d)
+        cp = rc(s_z.at[:, zz], r_z.at[d - 1], a1_s.at[2 + d], a1_r.at[2 + d], (c, tok_at(0, d)))
+        cp.start()
+        z1.append(cp)
 
     col = iota((1, POS), 1)
     for b in range(NT):
@@ -133,44 +148,13 @@
         onehot = (row == (iota((CAP, VIS), 1) + 1).astype(F32)).astype(F32).astype(BF16)
         send_e[b, :, 0:VIS] = onehot
     hot = send_e[:, :, 0:VIS].reshape(NT * CAP, VIS)
-    rows = dot(hot, normed[:, 0:D]).astype(BF16)
+    rows = dot(hot, normed[...]).astype(BF16)
     send_e[...] = rows.reshape(NT, CAP, D)
     recv_e[pl.ds(t, 1)] = send_e[pl.ds(t, 1)]
     e_cp = [
         rc(send_e.at[tok_at(dy, dz)], recv_e.at[t], e_s.at[i], e_r.at[i], (c, tok_at(dy, dz)))
         for i, (dy, dz) in enumerate(offsets)
     ]
-
-    top8 = m_send[...]
-    for i, cp in enumerate(m_cp):
-        cp.wait_recv()
-    for i in range(len(m_cp)):
-        top8 = jnp.maximum(top8, m_recv[i])
-    m_send_done = m_cp
-    for cp in m_send_done:
-        cp.wait_send()
-    m_send[...] = top8
-
-    y1, z1 = [], []
-    for d in (1, 3, 2, 0):
-        yy = mod(y + d)
-        lanes = pl.ds(pl.multiple_of(yy * 256, 256), 256)
-        pair = m_send[pl.ds(yy * 2, 2), :]
-        top = jnp.concatenate([pair[0:1, :], pair[1:2, :]], axis=1)
-        disp = jnp.exp(logits[:, lanes] - top).astype(BF16)
-        sums = dot(disp, normed[...], 0, 0)
-        s_y[pl.ds(yy, 1), :, 0:512] = sums[:, 0:512].astype(BF16)[None]
-        s_y[pl.ds(yy, 1), :, 512:] = sums[:, D:].astype(BF16)[None]
-        s_z[pl.ds(yy, 1)] = sums[:, 512:D].astype(BF16).reshape(1, R, SL, 512)
-        if d:
-            cp = rc(s_y.at[yy], r_y.at[d - 1], a1_s.at[d - 1], a1_r.at[d - 1], (c, tok_at(d, 0)))
-            cp.start()
-            y1.append(cp)
-    for d in (1, 3, 2):
-        zz = mod(z + d)
-        cp = rc(s_z.at[:, zz], r_z.at[d - 1], a1_s.at[2 + d], a1_r.at[2 + d], (c, tok_at(0, d)))
-        cp.start()
-        z1.append(cp)
 
     loads["w_proj"].wait()
     loads["w_back"].wait()
@@ -184,14 +168,27 @@
     filler[:, 0:256] = (mask[:, 0:256] + jnp.sin(angle)).astype(BF16)
     filler[:, 256:512] = (mask[:, 256:512] + jnp.cos(angle)).astype(BF16)
 
+    for cp in m_cp:
+        cp.wait_recv()
+    high = tops[:, 0, :]
+    shift = jnp.exp(high - jnp.max(high, axis=0, keepdims=True))
+    share = shift / jnp.sum(shift * tops[:, 1, :], axis=0, keepdims=True)
+    for k in range(8):
+        weight[k * 128 : (k + 1) * 128, :] = share[:, k * 128 : (k + 1) * 128].T
+
+    def weigh(e, dy, dz):
+        i = offsets.index((dy, dz)) + 1 if dy or dz else 0
+        return weight[pl.ds(pl.multiple_of(e * SL, SL), SL), i : i + 1]
+
     for cp in y1:
         cp.wait_recv()
     y2, own_y = [], None
     for d in (1, 3, 2, 0):
         at = pl.ds(pl.multiple_of(mod(z + d) * SL, SL), SL)
-        total = s_y[pl.ds(y, 1), at, :].astype(F32)[0]
+        e = y * R + mod(z + d)
+        total = weigh(e, 0, 0) * s_y[pl.ds(y, 1), at, :].astype(F32)[0]
         for i in range(3):
-            total = total + r_y[i, at, :].astype(F32)
+            total = total + weigh(e, i + 1, 0) * r_y[i, at, :].astype(F32)
         if d:
             s_y2[d - 1] = total.astype(BF16)
             cp = rc(s_y2.at[d - 1], r_y2.at[d - 1], a2_s.at[d - 1], a2_r.at[d - 1], (c, tok_at(0, d)))
@@ -204,9 +201,10 @@
     z2, own_z = [], None
     for d in (1, 3, 2, 0):
         yy = mod(y + d)
-        total = s_z[pl.ds(yy, 1), pl.ds(z, 1)].astype(F32)[0, 0]
+        e = yy * R + z
+        total = weigh(e, 0, 0) * s_z[pl.ds(yy, 1), pl.ds(z, 1)].astype(F32)[0, 0]
         for i in range(3):
-            total = total + r_z[i, pl.ds(yy, 1)].astype(F32)[0]
+            total = total + weigh(e, 0, i + 1) * r_z[i, pl.ds(yy, 1)].astype(F32)[0]
         if d:
             s_z2[d - 1] = total.astype(BF16)
             cp = rc(s_z2.at[d - 1], r_z2.at[d - 1], a2_s.at[2 + d], a2_r.at[2 + d], (c, tok_at(d, 0)))
@@ -222,9 +220,8 @@
     for i in range(3):
         own_y = own_y + r_y2[i].astype(F32)
         own_z = own_z + r_z2[i].astype(F32)
-    inverse = 1.0 / own_y[:, 512:513]
-    ag_b[pl.ds(c, 1), :, 0:512] = (own_y[:, 0:512] * inverse).astype(BF16)[None]
-    ag_b[pl.ds(c, 1), :, 512:] = (own_z * inverse).astype(BF16)[None]
+    ag_b[pl.ds(c, 1), :, 0:512] = own_y.astype(BF16)[None]
+    ag_b[pl.ds(c, 1), :, 512:] = own_z.astype(BF16)[None]
 
     b_cp = {}
     for dx in (1, 3, 2):
@@ -355,17 +352,17 @@
     def scores(block, into):
         q = recv_f[block, 0:HD, :]
         top = None
-        for k in range(NT * POS // KC):
-            s = dot(k_rows[k * KC : (k + 1) * KC, :], q)
-            into[k * KC : (k + 1) * KC, :] = s
-            m = jnp.max(s.reshape(KC // 8, 8, POS), axis=0)
+        for k in range(NT * POS // KS):
+            s = dot(k_rows[k * KS : (k + 1) * KS, :], q)
+            into[k * KS : (k + 1) * KS, :] = s
+            m = jnp.max(s.reshape(KS // 8, 8, POS), axis=0)
             top = m if top is None else jnp.maximum(top, m)
         return jnp.max(top, axis=0, keepdims=True)
 
     def finish(block, held, top):
         acc = jnp.zeros((HD + 16, POS), F32)
         for k in range(NT * POS // KC):
-            p = jnp.exp2(held[k * KC : (k + 1) * KC, :] - top).astype(BF16)
+            p = jnp.exp2((held[k * KC : (k + 1) * KC, :] - top).astype(BF16))
             acc = acc + dot(v_ext[:, k * KC : (k + 1) * KC], p)
         att[pl.ds(block, 1)] = (acc[0:HD] / acc[HD : HD + 1]).astype(BF16)[None]
 
@@ -405,7 +402,7 @@
     mixed = dot(recv_g[...].reshape(DD, POS), w_out[...], 0, 0)
     out_ref[...] = (mixed + dec_in[...].astype(F32)).astype(BF16)
 
-    for cp in e_cp + y1 + z1 + y2 + z2 + list(b_cp.values()) + list(fw.values()) + c_cp:
+    for cp in m_cp + e_cp + y1 + z1 + y2 + z2 + list(b_cp.values()) + list(fw.values()) + c_cp:
         cp.wait_send()
     for cp in list(d1y.values()) + list(d1z.values()) + d2 + f_cp:
         cp.wait_send()
@@ -428,21 +425,21 @@
         scratch_shapes=[
             V((VIS, D), BF16), V((D, SLOTS), BF16), V((D, HID), BF16), V((HID, D), BF16),
             V((D, DD), BF16), V((DD, 3 * DD), BF16), V((DD, DD), BF16),
-            V((VIS, D + EXT), BF16), V((VIS, SLOTS), F32), V((HID, DD), BF16), V((3 * DD, DD), BF16),
+            V((VIS, D), BF16), V((VIS, SLOTS), BF16), V((HID, DD), BF16), V((3 * DD, DD), BF16),
             V((2 * NT, POS), F32),
             V((NT, CAP, D), BF16), V((NT, CAP, D), BF16), V((POS, SLOTS), BF16), V((POS, DD), BF16),
             V((POS, DD), BF16),
-            V((8, 128), F32), V((NT - 1, 8, 128), F32),
-            V((R, 256, 512 + EXT), BF16), V((3, 256, 512 + EXT), BF16),
+            V((NT, 2, SLOTS), F32), V((SLOTS, NT), F32),
+            V((R, 256, 512), BF16), V((3, 256, 512), BF16),
             V((R, R, SL, 512), BF16), V((3, R, SL, 512), BF16),
-            V((3, SL, 512 + EXT), BF16), V((3, SL, 512 + EXT), BF16),
+            V((3, SL, 512), BF16), V((3, SL, 512), BF16),
             V((3, SL, 512), BF16), V((3, SL, 512), BF16),
             V((NC, SL, D), BF16), V((NC, SL, DD), BF16), V((NC - 1, SL, DD), BF16),
             V((R, R, SL, DD), BF16), V((HEADS, 3 * HD, POS), BF16), V((NT, 3 * HD, POS), BF16),
             V((NT * POS, HD), BF16), V((HD + 16, NT * POS), BF16),
             V((NT * POS, POS), F32), V((NT * POS, POS), F32),
             V((NT, HD, POS), BF16), V((HEADS, HD, POS), BF16),
-            dma(7), dma(15), dma(15), dma(15), dma(15), dma(6), dma(6), dma(6), dma(6),
+            dma(10), dma(15), dma(15), dma(15), dma(15), dma(6), dma(6), dma(6), dma(6),
             dma(7), dma(7), dma(7), dma(7), dma(30), dma(30), dma(15), dma(15), dma(15), dma(15), dma(15), dma(15),
         ],
         compiler_params=pltpu.CompilerParams(

time: 96.4 us -> 93.2 us (0.967)
  Pallas kernels: 94.5 us -> 91.3 us
    pallas_call x1, Pallas kernels: 94.5 us -> 91.3 us  [per_device(): pl.pallas_call(kernel, out_shape=jax.ShapeDtypeStruct((POS, DD), BF16), i...]
where the time goes in v3:
time: 93.2 us; the launch traced here: 93 us
  Pallas kernels  91.3 us (98%)
  local copies, waits for them, and re-layouts  1.67 us (2%)
    pallas_call x1, Pallas kernels, per_device(): pl.pallas_call(kernel, out_shape=jax.ShapeDtypeStruct((POS, DD), BF16), i...  91.3 us

profile of v3, /device:TPU:0, one launch (start us, length us, event | category | flops | bytes accessed | tf_op | source)
XLA Modules:
  0.0 93.0 jit_solution(2425266603661626108)
XLA Ops:
  0.0 91.3 %moe_mae.1 = bf16[256,512]{1,0:T(8,128)(2,1)} custom-call(bf16[512,1024]{1,0:T(8,128)(2,1)} %tokens_h.1, bf16[1024,1024]{1,0:T(8,128)(2,1)} %keys_h.1, bf16[1024,512]{1,0:T(8,128)(2,1)} %bitcast.2, bf16[512,1024]{1,0:T(8,128)(2,1)} %bitcast.3, bf16[1024,512]{1,0:T(8,128)(2,1)} %w_proj_h.1, s32[1,4096]{1,0:T(1,128)} %src_ref.1, bf16[512]{0:T(512)(128)(2,1)} %mask_ref.1, ...), custom_call_target="tpu_custom_call" | custom-call | tf_op jit(solution)/shard_map/moe_mae/pallas_call | solution.py:420
  91.3 1.7 %copy.12 = bf16[256,512]{1,0:T(8,128)(2,1)} copy(bf16[256,512]{1,0:T(8,128)(2,1)} %moe_mae.1) | data formatting | bytes 524288

commit v4 on v3

--- a/solution.py
+++ b/solution.py
@@ -25,8 +25,7 @@
 R = 4
 NT = 16
 NC = 8
-KS = 512
-KC = 512
+KC = 256
 
 
 def dot(a, b, ca=1, cb=0):
@@ -50,7 +49,7 @@
     normed, disp, w_bp, w_qkvt, ranks,
     send_e, recv_e, combine, filler, dec_in,
     tops, weight,
-    s_y, r_y, s_z, r_z, s_y2, r_y2, s_z2, r_z2,
+    s_y, r_y, s_z, r_z, p_all, q_all, s_y2, r_y2, s_z2, r_z2,
     ag_b, part_c, recv_c, ag_d, send_f, recv_f,
     k_rows, v_ext, sc0, sc1, att, recv_g,
     load_sem, e_s, e_r, m_s, m_r, a1_s, a1_r, a2_s, a2_r, b_s, b_r, c_s, c_r, d_s, d_r, f_s, f_r, g_s, g_r, q_s, q_r,
@@ -78,7 +77,8 @@
         loads[name] = pltpu.make_async_copy(h.at[at] if at else h, v.at[at] if at else v, load_sem.at[i])
         loads[name].start()
 
-    offsets = [(dy, dz) for dy in range(R) for dz in range(R) if dy or dz]
+    offsets = [(dy, dz) for dy in (2, 1, 3, 0) for dz in (2, 1, 3, 0) if dy or dz]
+    offsets.sort(key=lambda o: -min(o[0], R - o[0]) - min(o[1], R - o[1]))
 
     def tok_at(dy, dz):
         return mod(y + dy) * R + mod(z + dz)
@@ -116,21 +116,31 @@
     for cp in m_cp:
         cp.start()
 
-    y1, z1 = [], []
-    for d in (1, 3, 2, 0):
+    lo, hi = pl.ds(0, 256), pl.ds(256, 256)
+    one = {}
+    for d in (2, 1, 3, 0):
         yy = mod(y + d)
         sums = dot(disp[:, pl.ds(pl.multiple_of(yy * 256, 256), 256)], normed[...], 0, 0)
-        s_y[pl.ds(yy, 1)] = sums[:, 0:512].astype(BF16)[None]
+        s_y[pl.ds(yy, 1)] = sums[:, 0:512].astype(BF16).reshape(1, R, SL, 512)
         s_z[pl.ds(yy, 1)] = sums[:, 512:D].astype(BF16).reshape(1, R, SL, 512)
-        if d:
-            cp = rc(s_y.at[yy], r_y.at[d - 1], a1_s.at[d - 1], a1_r.at[d - 1], (c, tok_at(d, 0)))
-            cp.start()
-            y1.append(cp)
-    for d in (1, 3, 2):
-        zz = mod(z + d)
-        cp = rc(s_z.at[:, zz], r_z.at[d - 1], a1_s.at[2 + d], a1_r.at[2 + d], (c, tok_at(0, d)))
-        cp.start()
-        z1.append(cp)
+        if d == 2:
+            one["y_far_up"] = rc(s_y.at[yy, :, :, lo], r_y.at[0], a1_s.at[0], a1_r.at[0], (c, tok_at(1, 0)))
+            one["y_far_dn"] = rc(s_y.at[yy, :, :, hi], r_y.at[1], a1_s.at[1], a1_r.at[1], (c, tok_at(3, 0)))
+            one["y_far_up"].start()
+            one["y_far_dn"].start()
+        elif d == 1:
+            one["y_up"] = rc(s_y.at[yy, :, :, hi], r_y.at[2], a1_s.at[2], a1_r.at[2], (c, tok_at(1, 0)))
+            one["y_up"].start()
+        elif d == 3:
+            one["y_dn"] = rc(s_y.at[yy, :, :, lo], r_y.at[3], a1_s.at[3], a1_r.at[3], (c, tok_at(3, 0)))
+            one["y_dn"].start()
+    z_up, z_dn, z_far = mod(z + 1), mod(z + 3), mod(z + 2)
+    one["z_far_up"] = rc(s_z.at[:, z_far, :, lo], r_z.at[0], a1_s.at[6], a1_r.at[6], (c, tok_at(0, 1)))
+    one["z_far_dn"] = rc(s_z.at[:, z_far, :, hi], r_z.at[1], a1_s.at[7], a1_r.at[7], (c, tok_at(0, 3)))
+    one["z_up"] = rc(s_z.at[:, z_up, :, hi], r_z.at[2], a1_s.at[8], a1_r.at[8], (c, tok_at(0, 1)))
+    one["z_dn"] = rc(s_z.at[:, z_dn, :, lo], r_z.at[3], a1_s.at[9], a1_r.at[9], (c, tok_at(0, 3)))
+    for name in ("z_far_up", "z_far_dn", "z_up", "z_dn"):
+        one[name].start()
 
     col = iota((1, POS), 1)
     for b in range(NT):
@@ -173,22 +183,59 @@
     high = tops[:, 0, :]
     shift = jnp.exp(high - jnp.max(high, axis=0, keepdims=True))
     share = shift / jnp.sum(shift * tops[:, 1, :], axis=0, keepdims=True)
-    for k in range(8):
-        weight[k * 128 : (k + 1) * 128, :] = share[:, k * 128 : (k + 1) * 128].T
-
-    def weigh(e, dy, dz):
+    for e in range(0, NT, 2):
+        turned = share[:, e * SL : (e + 2) * SL].T
+        weight[e // R, e % R] = turned[0:SL, :]
+        weight[e // R, e % R + 1] = turned[SL:, :]
+
+    def column(dy, dz):
         i = offsets.index((dy, dz)) + 1 if dy or dz else 0
-        return weight[pl.ds(pl.multiple_of(e * SL, SL), SL), i : i + 1]
-
-    for cp in y1:
-        cp.wait_recv()
+        return slice(i, i + 1)
+
+    up_y, dn_y = mod(y + 1), mod(y + 3)
+
+    def relay(name, far, own, mine, theirs, out, i, dev):
+        one[name].wait_recv()
+        out[...] = (theirs * far[...].astype(F32) + mine * own.astype(F32)).astype(BF16)
+        cp = rc(out, q_all.at[i], a1_s.at[i], a1_r.at[i], dev)
+        cp.start()
+        return cp
+
+    def w_y(yy, dy):
+        return weight[pl.ds(yy, 1), :, :, column(dy, 0)][0]
+
+    def w_z(zz, dz):
+        return weight[:, pl.ds(zz, 1), :, column(0, dz)][:, 0]
+
+    one["y_q_up"] = relay(
+        "y_far_up", r_y.at[0], s_y[pl.ds(up_y, 1), :, :, 0:256][0], w_y(up_y, 0), w_y(up_y, 1),
+        p_all.at[0], 4, (c, tok_at(1, 0)),
+    )
+    one["y_q_dn"] = relay(
+        "y_far_dn", r_y.at[1], s_y[pl.ds(dn_y, 1), :, :, 256:512][0], w_y(dn_y, 0), w_y(dn_y, 3),
+        p_all.at[1], 5, (c, tok_at(3, 0)),
+    )
+    one["z_q_up"] = relay(
+        "z_far_up", r_z.at[0], s_z[:, pl.ds(z_up, 1), :, 0:256][:, 0], w_z(z_up, 0), w_z(z_up, 1),
+        p_all.at[2], 10, (c, tok_at(0, 1)),
+    )
+    one["z_q_dn"] = relay(
+        "z_far_dn", r_z.at[1], s_z[:, pl.ds(z_dn, 1), :, 256:512][:, 0], w_z(z_dn, 0), w_z(z_dn, 3),
+        p_all.at[3], 11, (c, tok_at(0, 3)),
+    )
+
+    for name in ("y_up", "y_dn", "y_q_up", "y_q_dn"):
+        one[name].wait_recv()
     y2, own_y = [], None
     for d in (1, 3, 2, 0):
-        at = pl.ds(pl.multiple_of(mod(z + d) * SL, SL), SL)
-        e = y * R + mod(z + d)
-        total = weigh(e, 0, 0) * s_y[pl.ds(y, 1), at, :].astype(F32)[0]
-        for i in range(3):
-            total = total + weigh(e, i + 1, 0) * r_y[i, at, :].astype(F32)
+        zz = mod(z + d)
+        w = weight[pl.ds(y, 1), pl.ds(zz, 1)][0, 0]
+        own = s_y[pl.ds(y, 1), pl.ds(zz, 1)][0, 0].astype(F32) * w[:, 0:1]
+        left = own[:, 0:256] + q_all[4, pl.ds(zz, 1)][0].astype(F32)
+        left = left + w[:, column(3, 0)] * r_y[3, pl.ds(zz, 1)][0].astype(F32)
+        right = own[:, 256:512] + q_all[5, pl.ds(zz, 1)][0].astype(F32)
+        right = right + w[:, column(1, 0)] * r_y[2, pl.ds(zz, 1)][0].astype(F32)
+        total = jnp.concatenate([left, right], axis=1)
         if d:
             s_y2[d - 1] = total.astype(BF16)
             cp = rc(s_y2.at[d - 1], r_y2.at[d - 1], a2_s.at[d - 1], a2_r.at[d - 1], (c, tok_at(0, d)))
@@ -196,15 +243,18 @@
             y2.append(cp)
         else:
             own_y = total
-    for cp in z1:
-        cp.wait_recv()
+    for name in ("z_up", "z_dn", "z_q_up", "z_q_dn"):
+        one[name].wait_recv()
     z2, own_z = [], None
     for d in (1, 3, 2, 0):
         yy = mod(y + d)
-        e = yy * R + z
-        total = weigh(e, 0, 0) * s_z[pl.ds(yy, 1), pl.ds(z, 1)].astype(F32)[0, 0]
-        for i in range(3):
-            total = total + weigh(e, 0, i + 1) * r_z[i, pl.ds(yy, 1)].astype(F32)[0]
+        w = weight[pl.ds(yy, 1), pl.ds(z, 1)][0, 0]
+        own = s_z[pl.ds(yy, 1), pl.ds(z, 1)][0, 0].astype(F32) * w[:, 0:1]
+        left = own[:, 0:256] + q_all[10, pl.ds(yy, 1)][0].astype(F32)
+        left = left + w[:, column(0, 3)] * r_z[3, pl.ds(yy, 1)][0].astype(F32)
+        right = own[:, 256:512] + q_all[11, pl.ds(yy, 1)][0].astype(F32)
+        right = right + w[:, column(0, 1)] * r_z[2, pl.ds(yy, 1)][0].astype(F32)
+        total = jnp.concatenate([left, right], axis=1)
         if d:
             s_z2[d - 1] = total.astype(BF16)
             cp = rc(s_z2.at[d - 1], r_z2.at[d - 1], a2_s.at[2 + d], a2_r.at[2 + d], (c, tok_at(d, 0)))
@@ -278,7 +328,6 @@
         total = total + recv_c[i].astype(F32)
     ag_d[pl.ds(y, 1), pl.ds(z, 1)] = total.astype(BF16).reshape(1, 1, SL, DD)
 
-    lo, hi = pl.ds(0, 256), pl.ds(256, 256)
     d1y, d1z, d2 = {}, {}, []
     for d in (1, 3, 2):
         d1y[d] = rc(
@@ -349,22 +398,21 @@
 
     lax.fori_loop(0, NT, gather_keys, 0)
 
-    def scores(block, into):
-        q = recv_f[block, 0:HD, :]
-        top = None
-        for k in range(NT * POS // KS):
-            s = dot(k_rows[k * KS : (k + 1) * KS, :], q)
-            into[k * KS : (k + 1) * KS, :] = s
-            m = jnp.max(s.reshape(KS // 8, 8, POS), axis=0)
-            top = m if top is None else jnp.maximum(top, m)
-        return jnp.max(top, axis=0, keepdims=True)
-
-    def finish(block, held, top):
-        acc = jnp.zeros((HD + 16, POS), F32)
+    def turn(block, held, top, nxt, into):
+        q = recv_f[nxt, 0:HD, :]
+        acc, high = jnp.zeros((HD + 16, POS), F32), None
         for k in range(NT * POS // KC):
-            p = jnp.exp2((held[k * KC : (k + 1) * KC, :] - top).astype(BF16))
-            acc = acc + dot(v_ext[:, k * KC : (k + 1) * KC], p)
-        att[pl.ds(block, 1)] = (acc[0:HD] / acc[HD : HD + 1]).astype(BF16)[None]
+            at = slice(k * KC, (k + 1) * KC)
+            if into is not None:
+                s = dot(k_rows[at, :], q)
+                into[at, :] = s
+                m = jnp.max(s.reshape(KC // 8, 8, POS), axis=0)
+                high = m if high is None else jnp.maximum(high, m)
+            if held is not None:
+                acc = acc + dot(v_ext[:, at], jnp.exp2((held[at, :] - top).astype(BF16)))
+        if held is not None:
+            att[pl.ds(block, 1)] = (acc[0:HD] / acc[HD : HD + 1]).astype(BF16)[None]
+        return jnp.max(high, axis=0, keepdims=True)
 
     def g_copy(i, block):
         return rc(att.at[block], recv_g.at[t], g_s.at[i], g_r.at[i], (c, block))
@@ -380,17 +428,15 @@
             q_copy(i).wait_recv()
 
     await_q(0)
-    top0 = scores(at_step(0), sc0)
+    top0 = turn(None, None, None, at_step(0), sc0)
 
     def two(j, top0):
         i = 2 * j
         await_q(i + 1)
-        top1 = scores(at_step(i + 1), sc1)
-        finish(at_step(i), sc0, top0)
+        top1 = turn(at_step(i), sc0, top0, at_step(i + 1), sc1)
         send_block(i, at_step(i))
         await_q(i + 2)
-        nxt = scores(at_step(lax.rem(i + 2, NT)), sc0)
-        finish(at_step(i + 1), sc1, top1)
+        nxt = turn(at_step(i + 1), sc1, top1, at_step(lax.rem(i + 2, NT)), sc0)
         send_block(i + 1, at_step(i + 1))
         return nxt
 
@@ -402,7 +448,7 @@
     mixed = dot(recv_g[...].reshape(DD, POS), w_out[...], 0, 0)
     out_ref[...] = (mixed + dec_in[...].astype(F32)).astype(BF16)
 
-    for cp in m_cp + e_cp + y1 + z1 + y2 + z2 + list(b_cp.values()) + list(fw.values()) + c_cp:
+    for cp in m_cp + e_cp + list(one.values()) + y2 + z2 + list(b_cp.values()) + list(fw.values()) + c_cp:
         cp.wait_send()
     for cp in list(d1y.values()) + list(d1z.values()) + d2 + f_cp:
         cp.wait_send()
@@ -429,9 +475,10 @@
             V((2 * NT, POS), F32),
             V((NT, CAP, D), BF16), V((NT, CAP, D), BF16), V((POS, SLOTS), BF16), V((POS, DD), BF16),
             V((POS, DD), BF16),
-            V((NT, 2, SLOTS), F32), V((SLOTS, NT), F32),
-            V((R, 256, 512), BF16), V((3, 256, 512), BF16),
-            V((R, R, SL, 512), BF16), V((3, R, SL, 512), BF16),
+            V((NT, 2, SLOTS), F32), V((R, R, SL, NT), F32),
+            V((R, R, SL, 512), BF16), V((4, R, SL, 256), BF16),
+            V((R, R, SL, 512), BF16), V((4, R, SL, 256), BF16),
+            V((4, R, SL, 256), BF16), V((12, R, SL, 256), BF16),
             V((3, SL, 512), BF16), V((3, SL, 512), BF16),
             V((3, SL, 512), BF16), V((3, SL, 512), BF16),
             V((NC, SL, D), BF16), V((NC, SL, DD), BF16), V((NC - 1, SL, DD), BF16),
@@ -439,7 +486,7 @@
             V((NT * POS, HD), BF16), V((HD + 16, NT * POS), BF16),
             V((NT * POS, POS), F32), V((NT * POS, POS), F32),
             V((NT, HD, POS), BF16), V((HEADS, HD, POS), BF16),
-            dma(10), dma(15), dma(15), dma(15), dma(15), dma(6), dma(6), dma(6), dma(6),
+            dma(10), dma(15), dma(15), dma(15), dma(15), dma(12), dma(12), dma(6), dma(6),
             dma(7), dma(7), dma(7), dma(7), dma(30), dma(30), dma(15), dma(15), dma(15), dma(15), dma(15), dma(15),
         ],
         compiler_params=pltpu.CompilerParams(

time: 93.2 us -> 88.9 us (0.954)
  Pallas kernels: 91.3 us -> 87 us
    pallas_call x1, Pallas kernels: 91.3 us -> 87 us  [per_device(): pl.pallas_call(kernel, out_shape=jax.ShapeDtypeStruct((POS, DD), BF16), i...]
where the time goes in v4:
time: 88.9 us; the launch traced here: 88.7 us
  Pallas kernels  87 us (98%)
  local copies, waits for them, and re-layouts  1.67 us (2%)
    pallas_call x1, Pallas kernels, per_device(): pl.pallas_call(kernel, out_shape=jax.ShapeDtypeStruct((POS, DD), BF16), i...  87 us

profile of v4, /device:TPU:0, one launch (start us, length us, event | category | flops | bytes accessed | tf_op | source)
XLA Modules:
  0.0 88.7 jit_solution(8207966269974174042)
XLA Ops:
  0.0 87.0 %moe_mae.1 = bf16[256,512]{1,0:T(8,128)(2,1)} custom-call(bf16[512,1024]{1,0:T(8,128)(2,1)} %tokens_h.1, bf16[1024,1024]{1,0:T(8,128)(2,1)} %keys_h.1, bf16[1024,512]{1,0:T(8,128)(2,1)} %bitcast.2, bf16[512,1024]{1,0:T(8,128)(2,1)} %bitcast.3, bf16[1024,512]{1,0:T(8,128)(2,1)} %w_proj_h.1, s32[1,4096]{1,0:T(1,128)} %src_ref.1, bf16[512]{0:T(512)(128)(2,1)} %mask_ref.1, ...), custom_call_target="tpu_custom_call" | custom-call | tf_op jit(solution)/shard_map/moe_mae/pallas_call | solution.py:466
  87.0 1.7 %copy.12 = bf16[256,512]{1,0:T(8,128)(2,1)} copy(bf16[256,512]{1,0:T(8,128)(2,1)} %moe_mae.1) | data formatting | bytes 524288

commit v5 on v4

--- a/solution.py
+++ b/solution.py
@@ -14,6 +14,7 @@
 BF16 = jnp.bfloat16
 D = 1024
 SL = 64
+SH = 32
 SLOTS = 1024
 DD = 512
 VIS = 512
@@ -226,6 +227,11 @@
 
     for name in ("y_up", "y_dn", "y_q_up", "y_q_dn"):
         one[name].wait_recv()
+    def two(src, dst, i, h, base, dev):
+        cp = rc(src.at[i, h], dst.at[i, h], a2_s.at[base + i], a2_r.at[base + i], dev)
+        cp.start()
+        return cp
+
     y2, own_y = [], None
     for d in (1, 3, 2, 0):
         zz = mod(z + d)
@@ -237,10 +243,8 @@
         right = right + w[:, column(1, 0)] * r_y[2, pl.ds(zz, 1)][0].astype(F32)
         total = jnp.concatenate([left, right], axis=1)
         if d:
-            s_y2[d - 1] = total.astype(BF16)
-            cp = rc(s_y2.at[d - 1], r_y2.at[d - 1], a2_s.at[d - 1], a2_r.at[d - 1], (c, tok_at(0, d)))
-            cp.start()
-            y2.append(cp)
+            s_y2[d - 1] = total.astype(BF16).reshape(2, SH, 512)
+            y2.append(two(s_y2, r_y2, d - 1, 0, 0, (c, tok_at(0, d))))
         else:
             own_y = total
     for name in ("z_up", "z_dn", "z_q_up", "z_q_dn"):
@@ -256,51 +260,68 @@
         right = right + w[:, column(0, 1)] * r_z[2, pl.ds(yy, 1)][0].astype(F32)
         total = jnp.concatenate([left, right], axis=1)
         if d:
-            s_z2[d - 1] = total.astype(BF16)
-            cp = rc(s_z2.at[d - 1], r_z2.at[d - 1], a2_s.at[2 + d], a2_r.at[2 + d], (c, tok_at(d, 0)))
-            cp.start()
-            z2.append(cp)
+            s_z2[d - 1] = total.astype(BF16).reshape(2, SH, 512)
+            z2.append(two(s_z2, r_z2, d - 1, 0, 3, (c, tok_at(d, 0))))
         else:
             own_z = total
-
-    for cp in y2 + z2:
-        cp.wait_recv()
+    late = [two(s_y2, r_y2, d - 1, 1, 6, (c, tok_at(0, d))) for d in (1, 3, 2)]
+    late += [two(s_z2, r_z2, d - 1, 1, 9, (c, tok_at(d, 0))) for d in (1, 3, 2)]
+    second = [y2 + z2, late]
+
+    b_cp, fw = {}, {}
+    partner = (clip_at(0, 1), t)
+    for h in (0, 1):
+        for cp in second[h]:
+            cp.wait_recv()
+        at = slice(h * SH, (h + 1) * SH)
+        left, right = own_y[at], own_z[at]
+        for i in range(3):
+            left = left + r_y2[i, h].astype(F32)
+            right = right + r_z2[i, h].astype(F32)
+        ag_b[h, pl.ds(c, 1), :, 0:512] = left.astype(BF16)[None]
+        ag_b[h, pl.ds(c, 1), :, 512:] = right.astype(BF16)[None]
+        held = ag_b.at[h, c]
+        for dx in (1, 3, 2):
+            i = h * 7 + dx - 1
+            b_cp[h, dx] = rc(held, held, b_s.at[i], b_r.at[i], (clip_at(dx, 0), t))
+            b_cp[h, dx].start()
+        fw[h, 0] = rc(held, held, b_s.at[h * 7 + 3], b_r.at[h * 7 + 3], partner)
+        fw[h, 0].start()
     for cp in e_cp:
         cp.start()
-    for i in range(3):
-        own_y = own_y + r_y2[i].astype(F32)
-        own_z = own_z + r_z2[i].astype(F32)
-    ag_b[pl.ds(c, 1), :, 0:512] = own_y.astype(BF16)[None]
-    ag_b[pl.ds(c, 1), :, 512:] = own_z.astype(BF16)[None]
-
-    b_cp = {}
-    for dx in (1, 3, 2):
-        b_cp[dx] = rc(ag_b.at[c], ag_b.at[c], b_s.at[dx - 1], b_r.at[dx - 1], (clip_at(dx, 0), t))
-        b_cp[dx].start()
-    partner = (clip_at(0, 1), t)
-    fw = {0: rc(ag_b.at[c], ag_b.at[c], b_s.at[3], b_r.at[3], partner)}
-    fw[0].start()
     loads["w_in"].wait()
-    c_cp = []
-    for step, dx in enumerate((0, 1, 3, 2)):
+    c_cp = [[], []]
+
+    def hand_over(h):
+        for dx in (1, 3, 2):
+            b_cp[h, dx].wait_recv()
+            held = ag_b.at[h, mod(x + R - dx) * 2 + co]
+            i = h * 7 + 3 + dx
+            fw[h, dx] = rc(held, held, b_s.at[i], b_r.at[i], partner)
+            fw[h, dx].start()
+
+    def expert(h, dx):
         chip = mod(x + R - dx)
-        if dx:
-            b_cp[dx].wait_recv()
-            held = ag_b.at[chip * 2 + co]
-            fw[dx] = rc(held, held, b_s.at[3 + dx], b_r.at[3 + dx], partner)
-            fw[dx].start()
-        fw[dx].wait_recv()
-        rows = ag_b[pl.ds(chip * 2, 2)].reshape(2 * SL, D)
+        fw[h, dx].wait_recv()
+        rows = ag_b[h, pl.ds(chip * 2, 2)].reshape(2 * SH, D)
         hidden = jax.nn.gelu(dot(rows, w_in[...])).astype(BF16)
-        part_c[pl.ds(chip * 2, 2)] = dot(hidden, w_bp[...]).astype(BF16).reshape(2, SL, DD)
+        part_c[h, pl.ds(chip * 2, 2)] = dot(hidden, w_bp[...]).astype(BF16).reshape(2, SH, DD)
         for f in (0, 1):
             if dx == 0 and f == 0:
                 continue
             i = ((R - dx) % R) * 2 + f - 1
             to = clip_at(R - dx, f)
-            cp = rc(part_c.at[to], recv_c.at[i], c_s.at[i], c_r.at[i], (to, t))
+            cp = rc(part_c.at[h, to], recv_c.at[h, i], c_s.at[h * 7 + i], c_r.at[h * 7 + i], (to, t))
             cp.start()
-            c_cp.append(cp)
+            c_cp[h].append(cp)
+
+    expert(0, 0)
+    expert(1, 0)
+    hand_over(0)
+    hand_over(1)
+    for h in (0, 1):
+        for dx in (1, 3, 2):
+            expert(h, dx)
 
     for cp in e_cp:
         cp.wait_recv()
@@ -321,38 +342,36 @@
     place_hot = (target == square1.astype(F32)).astype(F32).astype(BF16)
     combine[...] = dot(place_hot, comb).astype(BF16)
 
-    for cp in c_cp:
-        cp.wait_recv()
-    total = part_c[pl.ds(c, 1)].astype(F32)[0]
-    for i in range(NC - 1):
-        total = total + recv_c[i].astype(F32)
-    ag_d[pl.ds(y, 1), pl.ds(z, 1)] = total.astype(BF16).reshape(1, 1, SL, DD)
-
-    d1y, d1z, d2 = {}, {}, []
-    for d in (1, 3, 2):
-        d1y[d] = rc(
-            ag_d.at[y, z, :, lo], ag_d.at[y, z, :, lo], d_s.at[d - 1], d_r.at[d - 1], (c, tok_at(d, 0))
-        )
-        d1y[d].start()
-        d1z[d] = rc(
-            ag_d.at[y, z, :, hi], ag_d.at[y, z, :, hi], d_s.at[2 + d], d_r.at[2 + d], (c, tok_at(0, d))
-        )
-        d1z[d].start()
-    for d in (0, 1, 3, 2):
-        if d:
-            d1y[d].wait_recv()
-            d1z[d].wait_recv()
+    d1, d2 = {}, []
+
+    def spread(h, key, src, dev):
+        i = h * 30 + len([k for k in d1 if k[0] == h])
+        d1[(h,) + key] = rc(src, src, d_s.at[i], d_r.at[i], dev)
+        d1[(h,) + key].start()
+
+    def onward(h, d):
         ya, za = mod(y + R - d), mod(z + R - d)
         for e in (1, 3, 2):
-            i = 6 + d * 6 + (e - 1) * 2
-            cp = rc(ag_d.at[ya, z, :, lo], ag_d.at[ya, z, :, lo], d_s.at[i], d_r.at[i], (c, tok_at(0, e)))
-            cp.start()
-            d2.append(cp)
-            cp = rc(
-                ag_d.at[y, za, :, hi], ag_d.at[y, za, :, hi], d_s.at[i + 1], d_r.at[i + 1], (c, tok_at(e, 0))
-            )
-            cp.start()
-            d2.append(cp)
+            spread(h, ("y", d, e), ag_d.at[ya, z, h, :, lo], (c, tok_at(0, e)))
+            spread(h, ("z", d, e), ag_d.at[y, za, h, :, hi], (c, tok_at(e, 0)))
+
+    for h in (0, 1):
+        for cp in c_cp[h]:
+            cp.wait_recv()
+        total = part_c[h, pl.ds(c, 1)].astype(F32)[0]
+        for i in range(NC - 1):
+            total = total + recv_c[h, i].astype(F32)
+        ag_d[pl.ds(y, 1), pl.ds(z, 1), h] = total.astype(BF16).reshape(1, 1, SH, DD)
+        for d in (1, 3, 2):
+            spread(h, ("y", d), ag_d.at[y, z, h, :, lo], (c, tok_at(d, 0)))
+            spread(h, ("z", d), ag_d.at[y, z, h, :, hi], (c, tok_at(0, d)))
+        onward(h, 0)
+    for h in (0, 1):
+        for d in (1, 3, 2):
+            d1[h, "y", d].wait_recv()
+            d1[h, "z", d].wait_recv()
+            onward(h, d)
+    d2 = [cp for key, cp in d1.items() if len(key) == 4]
     for cp in d2:
         cp.wait_recv()
 
@@ -362,12 +381,9 @@
     dec_in[...] = held.astype(BF16)
     dec_normed = layer_norm(held).astype(BF16)
     scale = math.log2(math.e) / math.sqrt(HD)
-    for k in range(3):
+    for k in (1, 2):
         part = dot(w_qkvt[k * DD : (k + 1) * DD, :], dec_normed, 1, 1)
-        if k == 0:
-            part = part * scale
         send_f[:, k * HD : (k + 1) * HD, :] = part.astype(BF16).reshape(HEADS, HD, POS)
-    recv_f[pl.ds(t, 1)] = send_f[pl.ds(t, 1)]
     f_cp = [
         rc(
             send_f.at[tok_at(dy, dz), HD:], recv_f.at[t, HD:], f_s.at[i], f_r.at[i], (c, tok_at(dy, dz))
@@ -377,6 +393,10 @@
     for cp in f_cp:
         cp.start()
 
+    part = dot(w_qkvt[0:DD, :], dec_normed, 1, 1) * scale
+    send_f[:, 0:HD, :] = part.astype(BF16).reshape(HEADS, HD, POS)
+    recv_f[pl.ds(t, 1)] = send_f[pl.ds(t, 1)]
+
     def at_step(i):
         return lax.rem(t + 1 + i, NT)
 
@@ -390,16 +410,13 @@
     for cp in f_cp:
         cp.wait_recv()
 
-    def gather_keys(s, _):
-        at = pl.ds(pl.multiple_of(s * POS, POS), POS)
-        k_rows[at, :] = recv_f[s, HD : 2 * HD, :].T
-        v_ext[0:HD, at] = recv_f[s, 2 * HD :, :]
-        return 0
-
-    lax.fori_loop(0, NT, gather_keys, 0)
+    for k in range(NT):
+        at = slice(k * POS, (k + 1) * POS)
+        k_rows[at, :] = recv_f[k, HD : 2 * HD, :].T
+        v_ext[0:HD, at] = recv_f[k, 2 * HD :, :]
 
     def turn(block, held, top, nxt, into):
-        q = recv_f[nxt, 0:HD, :]
+        q = None if into is None else recv_f[nxt, 0:HD, :]
         acc, high = jnp.zeros((HD + 16, POS), F32), None
         for k in range(NT * POS // KC):
             at = slice(k * KC, (k + 1) * KC)
@@ -412,35 +429,28 @@
                 acc = acc + dot(v_ext[:, at], jnp.exp2((held[at, :] - top).astype(BF16)))
         if held is not None:
             att[pl.ds(block, 1)] = (acc[0:HD] / acc[HD : HD + 1]).astype(BF16)[None]
-        return jnp.max(high, axis=0, keepdims=True)
+        return None if high is None else jnp.max(high, axis=0, keepdims=True)
 
     def g_copy(i, block):
         return rc(att.at[block], recv_g.at[t], g_s.at[i], g_r.at[i], (c, block))
 
-    def send_block(i, block):
-        @pl.when(i < NT - 1)
-        def _():
-            g_copy(i, block).start()
-
-    def await_q(i):
-        @pl.when(i < NT - 1)
-        def _():
-            q_copy(i).wait_recv()
-
-    await_q(0)
+    q_copy(0).wait_recv()
     top0 = turn(None, None, None, at_step(0), sc0)
 
-    def two(j, top0):
+    def pair(j, top0):
         i = 2 * j
-        await_q(i + 1)
+        q_copy(i + 1).wait_recv()
         top1 = turn(at_step(i), sc0, top0, at_step(i + 1), sc1)
-        send_block(i, at_step(i))
-        await_q(i + 2)
-        nxt = turn(at_step(i + 1), sc1, top1, at_step(lax.rem(i + 2, NT)), sc0)
-        send_block(i + 1, at_step(i + 1))
+        g_copy(i, at_step(i)).start()
+        q_copy(i + 2).wait_recv()
+        nxt = turn(at_step(i + 1), sc1, top1, at_step(i + 2), sc0)
+        g_copy(i + 1, at_step(i + 1)).start()
         return nxt
 
-    lax.fori_loop(0, NT // 2, two, top0)
+    top0 = lax.fori_loop(0, NT // 2 - 1, pair, top0)
+    top1 = turn(at_step(NT - 2), sc0, top0, at_step(NT - 1), sc1)
+    g_copy(NT - 2, at_step(NT - 2)).start()
+    turn(at_step(NT - 1), sc1, top1, None, None)
     recv_g[pl.ds(t, 1)] = att[pl.ds(t, 1)]
     loads["w_out"].wait()
     for i in range(NT - 1):
@@ -448,9 +458,9 @@
     mixed = dot(recv_g[...].reshape(DD, POS), w_out[...], 0, 0)
     out_ref[...] = (mixed + dec_in[...].astype(F32)).astype(BF16)
 
-    for cp in m_cp + e_cp + list(one.values()) + y2 + z2 + list(b_cp.values()) + list(fw.values()) + c_cp:
+    for cp in m_cp + e_cp + list(one.values()) + second[0] + second[1] + list(b_cp.values()) + list(fw.values()) + c_cp[0] + c_cp[1]:
         cp.wait_send()
-    for cp in list(d1y.values()) + list(d1z.values()) + d2 + f_cp:
+    for cp in list(d1.values()) + f_cp:
         cp.wait_send()
     for i in range(NT - 1):
         g_copy(i, at_step(i)).wait_send()
@@ -479,15 +489,15 @@
             V((R, R, SL, 512), BF16), V((4, R, SL, 256), BF16),
             V((R, R, SL, 512), BF16), V((4, R, SL, 256), BF16),
             V((4, R, SL, 256), BF16), V((12, R, SL, 256), BF16),
-            V((3, SL, 512), BF16), V((3, SL, 512), BF16),
-            V((3, SL, 512), BF16), V((3, SL, 512), BF16),
-            V((NC, SL, D), BF16), V((NC, SL, DD), BF16), V((NC - 1, SL, DD), BF16),
-            V((R, R, SL, DD), BF16), V((HEADS, 3 * HD, POS), BF16), V((NT, 3 * HD, POS), BF16),
+            V((3, 2, SH, 512), BF16), V((3, 2, SH, 512), BF16),
+            V((3, 2, SH, 512), BF16), V((3, 2, SH, 512), BF16),
+            V((2, NC, SH, D), BF16), V((2, NC, SH, DD), BF16), V((2, NC - 1, SH, DD), BF16),
+            V((R, R, 2, SH, DD), BF16), V((HEADS, 3 * HD, POS), BF16), V((NT, 3 * HD, POS), BF16),
             V((NT * POS, HD), BF16), V((HD + 16, NT * POS), BF16),
             V((NT * POS, POS), F32), V((NT * POS, POS), F32),
             V((NT, HD, POS), BF16), V((HEADS, HD, POS), BF16),
-            dma(10), dma(15), dma(15), dma(15), dma(15), dma(12), dma(12), dma(6), dma(6),
-            dma(7), dma(7), dma(7), dma(7), dma(30), dma(30), dma(15), dma(15), dma(15), dma(15), dma(15), dma(15),
+            dma(10), dma(15), dma(15), dma(15), dma(15), dma(12), dma(12), dma(12), dma(12),
+            dma(14), dma(14), dma(14), dma(14), dma(60), dma(60), dma(15), dma(15), dma(15), dma(15), dma(15), dma(15),
         ],
         compiler_params=pltpu.CompilerParams(
             collective_id=0, has_side_effects=True, vmem_limit_bytes=60 << 20

time: 88.9 us -> 85.2 us (0.958)
  Pallas kernels: 87 us -> 83.3 us
    pallas_call x1, Pallas kernels: 87 us -> 83.3 us  [per_device(): pl.pallas_call(kernel, out_shape=jax.ShapeDtypeStruct((POS, DD), BF16), i...]
where the time goes in v5:
time: 85.2 us; the launch traced here: 85 us
  Pallas kernels  83.3 us (98%)
  local copies, waits for them, and re-layouts  1.67 us (2%)
    pallas_call x1, Pallas kernels, per_device(): pl.pallas_call(kernel, out_shape=jax.ShapeDtypeStruct((POS, DD), BF16), i...  83.3 us

profile of v5, /device:TPU:0, one launch (start us, length us, event | category | flops | bytes accessed | tf_op | source)
XLA Modules:
  0.0 85.0 jit_solution(14350586776185787893)
XLA Ops:
  0.0 83.3 %moe_mae.1 = bf16[256,512]{1,0:T(8,128)(2,1)} custom-call(bf16[512,1024]{1,0:T(8,128)(2,1)} %tokens_h.1, bf16[1024,1024]{1,0:T(8,128)(2,1)} %keys_h.1, bf16[1024,512]{1,0:T(8,128)(2,1)} %bitcast.2, bf16[512,1024]{1,0:T(8,128)(2,1)} %bitcast.3, bf16[1024,512]{1,0:T(8,128)(2,1)} %w_proj_h.1, s32[1,4096]{1,0:T(1,128)} %src_ref.1, bf16[512]{0:T(512)(128)(2,1)} %mask_ref.1, ...), custom_call_target="tpu_custom_call" | custom-call | tf_op jit(solution)/shard_map/moe_mae/pallas_call | solution.py:476
  83.3 1.7 %copy.12 = bf16[256,512]{1,0:T(8,128)(2,1)} copy(bf16[256,512]{1,0:T(8,128)(2,1)} %moe_mae.1) | data formatting | bytes 524288
